TPU v7x, 128 devices: a whole 4x4x4 slice. The times are simulated.
128 devices in a mesh: row: 8 (over x, core), mp: 16 (over y, z).
Axes of the slice: x: 4, y: 4, z: 4, core: 2. Of those that a mesh axis runs over, the one named last changes fastest.
Arguments:
- queries: bfloat16 [2560, 16384], P('row', 'mp'), may hold values from -16 to 16
- new_kv: bfloat16 [2560, 2048], P('row', 'mp'), may hold values from -9 to 9
- cache_keys: bfloat16 [512, 16, 512, 128], P('row', 'mp'), may hold values from -26 to 26
- cache_values: bfloat16 [512, 16, 512, 128], P('row', 'mp'), may hold values from -12 to 12
- cache_lens: int32 [512], P('row'), may hold values from 8 to 1019, as said below
- accepted: int32 [512], P('row'), may hold values from 0 to 5
- dest: int32 [512], P('row'), may hold values from 0 to 511, as said below
- out_weight: bfloat16 [16384, 16384], P('mp', 'row'), may hold values from -0.046875 to 0.046875
Outputs:
- mixed: bfloat16 [2560, 16384], P('mp', 'row')
- next_kv: bfloat16 [512, 5, 2048], P('row', None, 'mp')
Inputs may be any that keep to these rules, and one draw needn't show every extreme that they name: `cache_lens`: every beam's cache leaves room for its 5 new tokens. dest is a permutation of 0 to 511; of the beams in each aligned block of 64 beams, exactly 8 go to slots of each aligned block of 64 slots.
All inputs are finite; a program needn't handle non-finite values.
Results may differ from a plain program's by a relative error of at most 0.02.
Values may be sent and summed in bfloat16 or wider, within the bound.
A program may use at most 128 MiB of HBM per device.

v0:
```python
import jax
import jax.numpy as jnp
from jax import lax
from jax.sharding import PartitionSpec as P

masked_score = -1e30


def partner(block, axis, bit):
    count = lax.axis_size(axis)
    route = []
    for low in range(count):
        high = low | 1 << bit
        if high != low and high < count:
            route += [(low, high), (high, low)]
    return lax.ppermute(block, axis, route)


def head_slice(values, start, count):
    return lax.dynamic_slice_in_dim(values, start, count, 3)


def shards(queries, new_kv, cache_keys, cache_values, cache_lens, accepted, dest, out_weight):
    beams_here = cache_keys.shape[0]
    halves_held = cache_keys.shape[1]
    half_length = cache_keys.shape[2]
    head_size = cache_keys.shape[3]
    drafts = queries.shape[0] // beams_here
    heads_owned = queries.shape[1] // head_size
    kv_columns = new_kv.shape[1]
    mp_place = lax.axis_index("mp")
    lower_side = mp_place % 2 == 0
    partner_queries, partner_fresh = partner((queries, new_kv), "mp", 0)
    group_queries = jnp.where(
        lower_side,
        jnp.concatenate([queries, partner_queries], 1),
        jnp.concatenate([partner_queries, queries], 1),
    )
    fresh_pair = jnp.where(
        lower_side,
        jnp.concatenate([new_kv, partner_fresh], 1),
        jnp.concatenate([partner_fresh, new_kv], 1),
    )
    group_heads = group_queries.shape[1] // head_size
    sides = (mp_place * halves_held + jnp.arange(halves_held, dtype=jnp.int32)) % 2
    query_block = group_queries.reshape(beams_here, drafts, group_heads, head_size)
    fresh_block = fresh_pair.reshape(beams_here, drafts, 2, head_size)
    fresh_keys = fresh_block[:, :, 0]
    fresh_values = fresh_block[:, :, 1]
    scale = head_size ** (-0.5)
    cache_scores = (
        jnp.einsum("btjd,bsid->bstji", query_block, cache_keys, preferred_element_type=jnp.float32)
        * scale
    )
    fresh_scores = (
        jnp.einsum("btjd,bud->btju", query_block, fresh_keys, preferred_element_type=jnp.float32)
        * scale
    )
    spots = sides[:, None] * half_length + jnp.arange(half_length, dtype=jnp.int32)[None, :]
    cache_valid = (spots[None] < cache_lens[:, None, None])[:, :, None, None, :]
    order = jnp.arange(drafts, dtype=jnp.int32)
    fresh_side = (cache_lens[:, None] + order[None, :]) // half_length
    causal = order[:, None] >= order[None, :]
    fresh_valid = (
        causal[None, None] & (fresh_side[:, None, None, :] == sides[None, :, None, None])
    )[:, :, :, None, :]
    cache_masked = jnp.where(cache_valid, cache_scores, masked_score)
    fresh_masked = jnp.where(fresh_valid, fresh_scores[:, None], masked_score)
    highest = jnp.maximum(jnp.max(cache_masked, -1), jnp.max(fresh_masked, -1))
    cache_weights = jnp.where(cache_valid, jnp.exp(cache_masked - highest[..., None]), 0.0).astype(
        jnp.bfloat16
    )
    fresh_weights = jnp.where(fresh_valid, jnp.exp(fresh_masked - highest[..., None]), 0.0).astype(
        jnp.bfloat16
    )
    partial_value = jnp.einsum(
        "bstji,bsid->bstjd", cache_weights, cache_values, preferred_element_type=jnp.float32
    )
    partial_value = partial_value + jnp.einsum(
        "bstju,bud->bstjd", fresh_weights, fresh_values, preferred_element_type=jnp.float32
    )
    weight_mass = jnp.sum(cache_weights.astype(jnp.float32), -1) + jnp.sum(
        fresh_weights.astype(jnp.float32), -1
    )
    own_start = jnp.where(lower_side, 0, heads_owned).astype(jnp.int32)
    other_start = heads_owned - own_start
    got_partial, got_highest, got_mass = partner(
        (
            head_slice(partial_value, other_start, heads_owned),
            head_slice(highest, other_start, heads_owned),
            head_slice(weight_mass, other_start, heads_owned),
        ),
        "mp",
        0,
    )
    own_partial = head_slice(partial_value, own_start, heads_owned)
    own_highest = head_slice(highest, own_start, heads_owned)
    own_mass = head_slice(weight_mass, own_start, heads_owned)
    partial_value = jnp.where(
        lower_side,
        jnp.concatenate([own_partial, got_partial], 1),
        jnp.concatenate([got_partial, own_partial], 1),
    )
    highest = jnp.where(
        lower_side,
        jnp.concatenate([own_highest, got_highest], 1),
        jnp.concatenate([got_highest, own_highest], 1),
    )
    weight_mass = jnp.where(
        lower_side,
        jnp.concatenate([own_mass, got_mass], 1),
        jnp.concatenate([got_mass, own_mass], 1),
    )
    summit = jnp.max(highest, 1)
    factor = jnp.exp(highest - summit[:, None])
    numer = jnp.sum(factor[..., None] * partial_value, 1)
    denom = jnp.sum(factor * weight_mass, 1)
    attention = (
        (numer / denom[..., None])
        .astype(jnp.bfloat16)
        .reshape(beams_here * drafts, heads_owned * head_size)
    )
    projected = jnp.dot(
        lax.all_gather(attention, "row", axis=0, tiled=True),
        out_weight,
        preferred_element_type=jnp.float32,
    )
    rows_owned = projected.shape[0] // lax.axis_size("mp")
    totals = lax.psum(projected.astype(jnp.bfloat16), "mp").astype(jnp.float32)
    owned_rows = lax.dynamic_slice_in_dim(totals, mp_place * rows_owned, rows_owned, 0)
    mixed = owned_rows.astype(jnp.bfloat16)
    fresh_rows = new_kv.reshape(beams_here, drafts, kv_columns)
    kept_mask = order[None, :] < accepted[:, None]
    kept_rows = jnp.where(kept_mask[..., None], fresh_rows, jnp.zeros_like(fresh_rows)).reshape(
        beams_here, drafts * kv_columns
    )
    blocks = lax.axis_size("row")
    share_count = beams_here // blocks
    target = dest // beams_here
    landing = dest % beams_here
    beam_index = jnp.arange(beams_here, dtype=jnp.int32)
    earlier = (target[None, :] == target[:, None]) & (beam_index[None, :] < beam_index[:, None])
    position = jnp.sum(earlier.astype(jnp.int32), 1)
    send_slot = target * share_count + position
    picker = send_slot[None, :] == beam_index[:, None]
    outgoing = jnp.dot(
        picker.astype(jnp.bfloat16), kept_rows, preferred_element_type=jnp.float32
    ).astype(jnp.bfloat16)
    outgoing = outgoing.reshape(blocks, share_count, drafts * kv_columns)
    labels = jnp.sum(jnp.where(picker, landing[None, :], 0), 1).reshape(blocks, share_count)
    arrived, arrived_labels = (
        lax.all_to_all(outgoing, "row", split_axis=0, concat_axis=0, tiled=True),
        lax.all_to_all(labels, "row", split_axis=0, concat_axis=0, tiled=True),
    )
    arrived = arrived.reshape(beams_here, drafts * kv_columns)
    arrived_labels = arrived_labels.reshape(beams_here)
    placer = (arrived_labels[None, :] == beam_index[:, None]).astype(jnp.bfloat16)
    next_kv = jnp.dot(placer, arrived, preferred_element_type=jnp.float32).astype(jnp.bfloat16)
    next_kv = next_kv.reshape(beams_here, drafts, kv_columns)
    return (mixed, next_kv)


def solution(mesh):
    placed = (
        P("row", "mp"),
        P("row", "mp"),
        P("row", "mp", None, None),
        P("row", "mp", None, None),
        P("row"),
        P("row"),
        P("row"),
        P("mp", "row"),
    )
    return jax.shard_map(
        shards,
        mesh=mesh,
        in_specs=placed,
        out_specs=(P("mp", "row"), P("row", None, "mp")),
        check_vma=False,
    )
```

profile of v0, /device:TPU:14, one launch (start us, length us, event | category | flops | bytes accessed | tf_op | source)
XLA Modules:
  0.0 306.5 jit_solution(3005448129393214941)
XLA Ops:
  7.2 0.0 all-gather.2.cloned.1.call-start
  7.2 2.0 collective-permute-start
  9.2 0.1 collective-permute-start.1
  9.3 0.7 fusion.18
  10.1 0.7 broadcast_compare_fusion
  10.9 15.0 %collective-permute-done.1 = bf16[320,128]{1,0:T(8,128)(2,1)S(1)} collective-permute-done((bf16[320,128]{1,0:T(8,128)(2,1)}, bf16[320,128]{1,0:T(8,128)(2,1)S(1)}, u32[]{:S(2)}, u32[]{:S(2)}) %collective-permute-start.1) | collective-permute-done | bytes 81952 | tf_op jit(solution)/shard_map/ppermute | solution.py:16
  25.9 1.0 maximum_select_fusion.2
  27.0 0.2 fusion.26
  27.2 0.0 collective-permute-done
  27.2 1.8 fusion.10
  29.0 0.3 copy.56
  29.3 6.5 %fusion.1 = (f32[64,5,16]{2,1,0:T(8,128)S(1)}, f32[64,5,16,512]{3,2,1,0:T(8,128)S(1)}) fusion(pred[64,512]{1,0:T(8,128)(4,1)S(1)} %broadcast_compare_fusion, bf16[64,5,16,128]{3,2,1,0:T(8,128)(2,1)S(1)} %bitcast.96, bf16[64,1,512,128]{3,2,1,0:T(8,128)(2,1)} %param.10), kind=kOutput, calls=%fused_computation.5 | convolution fusion | flops 678947840 | bytes 20238336 | tf_op jit(solution)/shard_map/btjd,bsid->bstji/dot_general | solution.py:52
  35.8 0.0 copy-start
  35.8 3.2 %fusion.27 = (f32[64,5,16]{2,1,0:T(8,128)S(1)}, f32[64,5,16,5]{2,3,1,0:T(8,128)S(1)}) fusion(bf16[64,5,16,128]{3,2,1,0:T(8,128)(2,1)S(1)} %bitcast.97, bf16[64,5,1,128]{3,2,1,0:T(2,128)(2,1)S(1)} %get-tuple-element.23, pred[64,5,5]{2,1,0:T(8,128)(4,1)S(1)} %broadcast_and_fusion), kind=kOutput, calls=%fused_computation.78 | convolution fusion | flops 6625280 | bytes 1517120 | tf_op jit(solution)/shard_map/btjd,bud->btju/dot_general | solution.py:56
  39.0 1.5 convert_reduce_fusion.1
  40.6 5.6 %fusion.2 = f32[64,5,16,128]{3,2,1,0:T(8,128)S(1)} fusion(bf16[64,1,512,128]{3,2,1,0:T(8,128)(2,1)} %param.11, f32[64,5,16,512]{3,2,1,0:T(8,128)S(1)} %get-tuple-element.27, f32[64,5,16]{2,1,0:T(8,128)S(1)} %max.16, pred[64,512]{1,0:T(8,128)(4,1)S(1)} %broadcast_compare_fusion), kind=kOutput, calls=%fused_computation.6 | convolution fusion | flops 684195840 | bytes 21549056 | tf_op jit(solution)/shard_map/bstji,bsid->bstjd/dot_general | solution.py:76
  46.1 0.0 copy-done
  46.2 1.7 convolution_add_fusion
  47.9 1.3 dynamic-slice_bitcast_fusion.1
  49.1 1.7 collective-permute-start.3
  50.9 0.2 constant_dynamic-slice_fusion.2
  51.1 0.1 copy.41
  51.2 0.3 collective-permute-start.2
  51.5 6.7 %convert_reduce_fusion = f32[64,5,16]{2,1,0:T(8,128)S(1)} fusion(f32[64,5,16]{2,1,0:T(8,128)S(1)} %max.16, f32[64,5,16,512]{3,2,1,0:T(8,128)} %copy-done, pred[64,512]{1,0:T(8,128)(4,1)S(1)} %broadcast_compare_fusion), kind=kLoop, calls=%fused_computation.3 | loop fusion | flops 18344960 | bytes 10559488 | tf_op jit(solution)/shard_map/reduce_sum | solution.py:82
  58.2 0.0 copy-done.1
  58.3 0.2 constant_dynamic-slice_fusion.1
  58.5 0.1 copy.45
  58.6 1.8 collective-permute-start.4
  60.3 0.1 copy.40
  60.5 0.1 copy.44
  60.6 19.3 %collective-permute-done.2 = f32[64,1,5,8]{0,3,2,1:T(8,128)S(1)} collective-permute-done((f32[64,1,5,8]{0,3,2,1:T(8,128)S(1)}, f32[64,1,5,8]{0,3,2,1:T(8,128)S(1)}, u32[]{:S(2)}, u32[]{:S(2)}) %collective-permute-start.2) | collective-permute-done | bytes 10272 | tf_op jit(solution)/shard_map/ppermute | solution.py:16
  79.9 0.2 collective-permute-done.4
  80.1 0.2 copy.42
  80.3 0.1 copy.46
  80.5 0.0 collective-permute-done.3
  80.5 1.0 fusion.8
  81.5 0.4 divide_convert_fusion
  82.0 1.0 copy.69
  82.9 0.0 all-gather.2.cloned.1.call-update
  82.9 0.2 all-reduce.2.cloned.1.call-start
  83.2 36.4 %all-gather.2.cloned.1.call-done = bf16[2560,1024]{1,0:T(8,128)(2,1)} async-done(((bf16[320,1024]{1,0:T(8,128)(2,1)}), bf16[2560,1024]{1,0:T(8,128)(2,1)}) %all-gather.2.cloned.1.call-update) | async-done | bytes 5242896 | tf_op jit(solution)/shard_map/all_gather | solution.py:124
  119.6 16.6 %convolution_convert_fusion = bf16[2560,2048]{1,0:T(8,128)(2,1)} fusion(bf16[2560,1024]{1,0:T(8,128)(2,1)} %all-gather.2.cloned.1.call-done, bf16[1024,2048]{1,0:T(8,128)(2,1)} %param.15), kind=kOutput, calls=%fused_computation | convolution fusion | flops 10742661120 | bytes 19922944 | tf_op jit(solution)/shard_map/dot_general | solution.py:123
  136.1 0.0 all-reduce.2.cloned.1.call-update
  136.2 0.6 copy-done.4
  136.8 0.2 convert_reduce_fusion.2
  137.0 0.1 select_reduce_fusion
  137.1 0.7 all_to_all.9
  137.8 5.6 %all-to-all-start = ((s32[8,1,8]{2,1,0:T(1,128)}), s32[8,1,8]{2,1,0:T(1,128)S(1)}, u32[]{:S(2)}, u32[]{:S(2)}) async-start(s32[8,1,8]{2,1,0:T(1,128)} %bitcast.25), calls=%async_computation | async-start | bytes 8192 | tf_op jit(solution)/shard_map/all_to_all | solution.py:153
  143.4 0.0 copy-done.2
  143.4 0.1 reshape.269
  143.5 0.0 copy-done.3
  143.5 0.1 iota_compare_fusion
  143.6 0.1 broadcast_in_dim.102
  143.7 0.8 fusion.11
  144.5 2.0 all-to-all-done
  146.5 5.4 %all-to-all-start.1 = ((bf16[8,8,640]{2,1,0:T(8,128)(2,1)}), bf16[8,8,640]{2,1,0:T(8,128)(2,1)S(1)}, u32[]{:S(2)}, u32[]{:S(2)}) async-start(bf16[8,8,640]{2,1,0:T(8,128)(2,1)} %fusion.11), calls=%async_computation.1 | async-start | bytes 163840 | tf_op jit(solution)/shard_map/all_to_all | solution.py:152
  151.9 0.5 broadcast.179
  152.4 0.7 reduce.9
  153.1 0.1 eq.70
  153.1 2.4 all-to-all-done.1
  155.5 0.1 fusion.12
  155.6 0.7 copy.70
  156.3 141.3 %all-reduce.2.cloned.1.call-done = bf16[2560,2048]{1,0:T(8,128)(2,1)} async-done(((bf16[2560,2048]{1,0:T(8,128)(2,1)}), bf16[2560,2048]{1,0:T(8,128)(2,1)}) %all-reduce.2.cloned.1.call-update) | async-done | bytes 10485776 | tf_op jit(solution)/shard_map/psum | solution.py:129
  297.7 2.0 convert_convert_fusion
  (14 shorter events, 0.2 us)
Async XLA Ops:
  7.2 112.4 %all-gather.2.cloned.1.call-start = ((), (), s32[]{:S(2)}) async-start(), calls=%async_computation.2 | async-start | bytes 5898240 | tf_op jit(solution)/shard_map/all_gather | solution.py:124
  7.2 20.0 %collective-permute-start = (bf16[320,1024]{1,0:T(8,128)(2,1)}, bf16[320,1024]{1,0:T(8,128)(2,1)S(1)}, u32[]{:S(2)}, u32[]{:S(2)}) collective-permute-start(bf16[320,1024]{1,0:T(8,128)(2,1)} %param.8), channel_id=1, source_target_pairs={{0,1},{1,0},{2,3},{3,2},{4,5},{5,4},{6,7},{7,6},{8,9},{9,8},{10,11... | collective-permute-start | bytes 1966088 | tf_op jit(solution)/shard_map/ppermute | solution.py:16
  9.2 16.7 %collective-permute-start.1 = (bf16[320,128]{1,0:T(8,128)(2,1)}, bf16[320,128]{1,0:T(8,128)(2,1)S(1)}, u32[]{:S(2)}, u32[]{:S(2)}) collective-permute-start(bf16[320,128]{1,0:T(8,128)(2,1)} %param.9), channel_id=1, source_target_pairs={{0,1},{1,0},{2,3},{3,2},{4,5},{5,4},{6,7},{7,6},{8,9},{9,8},{10,11... | collective-permute-start | bytes 245768 | tf_op jit(solution)/shard_map/ppermute | solution.py:16
  35.8 10.3 %copy-start = (f32[64,5,16,512]{3,2,1,0:T(8,128)}, f32[64,5,16,512]{3,2,1,0:T(8,128)S(1)}, u32[]{:S(2)}) copy-start(f32[64,5,16,512]{3,2,1,0:T(8,128)S(1)} %get-tuple-element.27) | copy-start | bytes 31457284
  49.1 31.4 %collective-permute-start.3 = (f32[64,1,5,8,128]{4,3,2,0,1:T(8,128)}, f32[64,1,5,8,128]{4,3,2,0,1:T(8,128)S(1)}, u32[]{:S(2)}, u32[]{:S(2)}) collective-permute-start(f32[64,1,5,8,128]{4,3,2,0,1:T(8,128)} %get-tuple-element.17), channel_id=1, source_target_pairs={{0,1},{1,0},{2,3},{3,2},{4,5},{5,4},{6,7},{7,6},{8,9},{9,8},{10,11... | collective-permute-start | bytes 3932168 | tf_op jit(solution)/shard_map/ppermute | solution.py:16
  51.2 7.0 %copy-start.1 = (f32[64,5,16]{2,1,0:T(8,128)S(1)}, f32[64,5,16]{2,1,0:T(8,128)}, u32[]{:S(2)}) copy-start(f32[64,5,16]{2,1,0:T(8,128)} %convert_reduce_fusion.1) | copy-start | bytes 61444
  51.2 28.7 %collective-permute-start.2 = (f32[64,1,5,8]{0,3,2,1:T(8,128)S(1)}, f32[64,1,5,8]{0,3,2,1:T(8,128)S(1)}, u32[]{:S(2)}, u32[]{:S(2)}) collective-permute-start(f32[64,1,5,8]{0,3,2,1:T(8,128)S(1)} %bitcast.105), channel_id=1, source_target_pairs={{0,1},{1,0},{2,3},{3,2},{4,5},{5,4},{6,7},{7,6},{8,9},{9,8},{10,11... | collective-permute-start | bytes 30728 | tf_op jit(solution)/shard_map/ppermute | solution.py:16
  58.6 21.5 %collective-permute-start.4 = (f32[64,1,5,8]{0,3,2,1:T(8,128)S(1)}, f32[64,1,5,8]{0,3,2,1:T(8,128)S(1)}, u32[]{:S(2)}, u32[]{:S(2)}) collective-permute-start(f32[64,1,5,8]{0,3,2,1:T(8,128)S(1)} %bitcast.106), channel_id=1, source_target_pairs={{0,1},{1,0},{2,3},{3,2},{4,5},{5,4},{6,7},{7,6},{8,9},{9,8},{10,11... | collective-permute-start | bytes 30728 | tf_op jit(solution)/shard_map/ppermute | solution.py:16
  82.9 214.7 %all-reduce.2.cloned.1.call-start = ((), (), s32[]{:S(2)}) async-start(), calls=%async_computation.3 | async-start | bytes 20971520 | tf_op jit(solution)/shard_map/psum | solution.py:129
  136.1 0.7 copy-start.4
  136.1 7.3 %copy-start.2 = (bf16[320,128]{1,0:T(8,128)(2,1)S(1)}, bf16[320,128]{1,0:T(8,128)(2,1)}, u32[]{:S(2)}) copy-start(bf16[320,128]{1,0:T(8,128)(2,1)} %param.9) | copy-start | bytes 245764
  136.1 7.4 %copy-start.3 = (s32[64]{0:T(128)S(1)}, s32[64]{0:T(128)}, u32[]{:S(2)}) copy-start(s32[64]{0:T(128)} %param.13) | copy-start | bytes 772
  137.8 8.7 %all-to-all-start = ((s32[8,1,8]{2,1,0:T(1,128)}), s32[8,1,8]{2,1,0:T(1,128)S(1)}, u32[]{:S(2)}, u32[]{:S(2)}) async-start(s32[8,1,8]{2,1,0:T(1,128)} %bitcast.25), calls=%async_computation | async-start | bytes 8192 | tf_op jit(solution)/shard_map/all_to_all | solution.py:153
  146.5 9.0 %all-to-all-start.1 = ((bf16[8,8,640]{2,1,0:T(8,128)(2,1)}), bf16[8,8,640]{2,1,0:T(8,128)(2,1)S(1)}, u32[]{:S(2)}, u32[]{:S(2)}) async-start(bf16[8,8,640]{2,1,0:T(8,128)(2,1)} %fusion.11), calls=%async_computation.1 | async-start | bytes 163840 | tf_op jit(solution)/shard_map/all_to_all | solution.py:152
Sparse Core Ops, SparseCore 0:
  83.1 36.4 all-gather.1
  136.3 161.3 all-reduce.1
where the time goes:
time: 308 us; the launch traced here: 306 us
  waiting for transfers between devices  217 us (70%)
  matrix products  34.4 us (11%)
  starting transfers between devices  17.2 us (6%)
  other arithmetic  17.1 us (6%)
  between operations  14.3 us (5%)
  local copies, waits for them, and re-layouts  6.79 us (2%)
    psum x1, waiting for transfers between devices, shards(): totals = lax.psum(projected.astype(jnp.bfloat16), 'mp').astype(jnp.float32)  141 us
    all_gather x1, waiting for transfers between devices, shards(): lax.all_gather(attention, 'row', axis=0, tiled=True)  36.4 us
    ppermute x5, waiting for transfers between devices, partner(): return lax.ppermute(block, axis, route)  34.5 us
    dot_general x1, matrix products, shards(): jnp.dot(lax.all_gather(attention, 'row', axis=0, tiled=True), out_weight,...  16.6 us
    reduce_sum x1, other arithmetic, shards(): jnp.sum(cache_weights.astype(jnp.float32), -1)  6.68 us
    dot_general x1, matrix products, shards(): jnp.einsum('btjd,bsid->bstji', query_block, cache_keys, preferred_element...  6.47 us
  transfers between devices with their start and end apart: 9, of which 7 were waited for; matrix products, arithmetic and copies ran while one was open for 5% of the time, Pallas kernels for 0%

commit v1 on v0

--- a/solution.py
+++ b/solution.py
@@ -1,9 +1,298 @@
+import functools
+
 import jax
 import jax.numpy as jnp
 from jax import lax
+from jax.experimental import pallas as pl
+from jax.experimental.pallas import tpu as pltpu
 from jax.sharding import PartitionSpec as P
 
+MESH = pl.DeviceIdType.MESH
 masked_score = -1e30
+
+TREES = ((0, 2, 1, 3), (2, 1, 3, 0), (1, 3, 0, 2), (3, 0, 2, 1))
+STEP_BASE = (0, 8, 12, 14)
+LAG = 2
+
+
+def bits_of(place):
+    y, z = place // 4, place % 4
+    return (((y + 1) // 2) % 2, y // 2, ((z + 1) // 2) % 2, z // 2)
+
+
+def along(place, direction):
+    y, z = place // 4, place % 4
+    if direction == 0:
+        y = y + 1 - 2 * (y % 2)
+    elif direction == 1:
+        y = 3 - y
+    elif direction == 2:
+        z = z + 1 - 2 * (z % 2)
+    else:
+        z = 3 - z
+    return y * 4 + z
+
+
+def all_of(terms):
+    result = terms[0]
+    for term in terms[1:]:
+        result = jnp.logical_and(result, term)
+    return result
+
+
+def project_kernel(
+    attention, weight, fresh, keyed, mixed, next_kv,
+    gathered, weight_here, held, inbox, parcels, arrived,
+    local_sem, own_send, far_send, gather_recv, tree_send, tree_recv, parcel_send, parcel_recv,
+):
+    row, mp = lax.axis_index("row"), lax.axis_index("mp")
+    x, core = row // 2, row % 2
+    sibling = {"row": x * 2 + 1 - core, "mp": mp}
+    right = {"row": ((x + 1) % 4) * 2 + core, "mp": mp}
+    left = {"row": ((x + 3) % 4) * 2 + core, "mp": mp}
+    weight_copy = pltpu.make_async_copy(weight, weight_here, local_sem.at[0])
+    weight_copy.start()
+    own_copy = pltpu.make_async_copy(attention, gathered.at[0], local_sem.at[1])
+    own_copy.start()
+
+    barrier = pltpu.get_barrier_semaphore()
+    for step in range(1, 8):
+        pl.semaphore_signal(
+            barrier, inc=1, device_id={"row": (row + step) % 8, "mp": mp}, device_id_type=MESH
+        )
+    for direction in range(4):
+        pl.semaphore_signal(
+            barrier, inc=1, device_id={"row": row, "mp": along(mp, direction)}, device_id_type=MESH
+        )
+    pl.semaphore_wait(barrier, 11)
+
+    def remote(source, target, send_sem, recv_sem, device):
+        return pltpu.make_async_remote_copy(
+            src_ref=source, dst_ref=target, send_sem=send_sem, recv_sem=recv_sem,
+            device_id=device, device_id_type=MESH,
+        )
+
+    half = gathered.shape[1] // 2
+    own_copy.wait()
+    to_right = remote(gathered.at[0], gathered.at[3], own_send.at[0], gather_recv.at[3], right)
+    to_left = remote(gathered.at[0], gathered.at[2], own_send.at[1], gather_recv.at[2], left)
+    to_sibling = remote(gathered.at[0], gathered.at[1], own_send.at[2], gather_recv.at[1], sibling)
+    to_left.start()
+    to_right.start()
+    to_sibling.start()
+    pass_left = remote(
+        gathered.at[2, pl.ds(0, half)], gathered.at[6, pl.ds(0, half)], far_send.at[0], gather_recv.at[6], left
+    )
+    pass_right = remote(
+        gathered.at[3, pl.ds(half, half)], gathered.at[6, pl.ds(half, half)], far_send.at[1], gather_recv.at[8], right
+    )
+    share_right = remote(gathered.at[2], gathered.at[4], far_send.at[2], gather_recv.at[4], sibling)
+    share_left = remote(gathered.at[3], gathered.at[5], far_send.at[3], gather_recv.at[5], sibling)
+    share_far = remote(gathered.at[6], gathered.at[7], far_send.at[4], gather_recv.at[7], sibling)
+
+    place = lax.broadcasted_iota(jnp.int32, (64, 320), 0)
+    fresh_rows = fresh[...]
+    columns = []
+    for draft in range(5):
+        pick = (keyed[draft : draft + 1, :] == place).astype(jnp.bfloat16)
+        columns.append(
+            jnp.dot(pick, fresh_rows, preferred_element_type=jnp.float32).astype(jnp.bfloat16)
+        )
+    label = jnp.sum(
+        jnp.where(keyed[5:6, :] == place, keyed[6:7, :], 0).astype(jnp.float32), 1, keepdims=True
+    )
+    columns.append(jnp.broadcast_to(label, (64, 128)).astype(jnp.bfloat16))
+    for block in range(8):
+        for part, column in enumerate(columns):
+            parcels[block, :, pl.ds(part * 128, 128)] = column[block * 8 : block * 8 + 8]
+    own_parcel = pltpu.make_async_copy(parcels.at[row], arrived.at[row], local_sem.at[2])
+    own_parcel.start()
+    for step in range(1, 8):
+        target = (row + step) % 8
+        remote(
+            parcels.at[target], arrived.at[row], parcel_send.at[step], parcel_recv.at[row],
+            {"row": target, "mp": mp},
+        ).start()
+    weight_copy.wait()
+
+    rows_owned = mixed.shape[0]
+    width = held.shape[3]
+    my_bits = bits_of(mp)
+
+    def tree_message(tree, step, block):
+        order = TREES[tree]
+        rest = bits_of(block)
+        index = STEP_BASE[step]
+        for power, direction in enumerate(order[step + 1 :]):
+            index = index + rest[direction] * (1 << power)
+        return remote(
+            held.at[tree, block], inbox.at[tree, index], tree_send.at[tree, block],
+            tree_recv.at[tree, index], {"row": row, "mp": along(mp, order[step])},
+        ), index
+
+    def first_block(slot):
+        shift = jnp.where(slot < 2, 0, jnp.where(slot >= 6, 2, jnp.where(slot % 2 == 0, 1, 3)))
+        other = jnp.where(slot < 6, jnp.where(slot < 2, slot, jnp.where(slot >= 4, 1, 0)), slot - 6)
+        owner = ((x + shift) % 4) * 2 + jnp.where(other == 1, 1 - core, core)
+        return owner * 2
+
+    def iteration(turn, carry):
+        @pl.when(turn == 1)
+        def _():
+            to_sibling.wait_recv()
+
+        @pl.when(turn == 2)
+        def _():
+            to_left.wait_recv()
+            pass_left.start()
+            share_right.start()
+
+        @pl.when(turn == 3)
+        def _():
+            to_right.wait_recv()
+            pass_right.start()
+            share_left.start()
+
+        @pl.when(turn == 4)
+        def _():
+            share_right.wait_recv()
+
+        @pl.when(turn == 5)
+        def _():
+            share_left.wait_recv()
+
+        @pl.when(turn == 6)
+        def _():
+            pass_left.wait_recv()
+            pass_right.wait_recv()
+            share_far.start()
+
+        @pl.when(turn == 7)
+        def _():
+            share_far.wait_recv()
+
+        @pl.when(turn < 8)
+        def _():
+            base = first_block(turn)
+            for tree in range(4):
+                product = jnp.dot(
+                    gathered[turn], weight_here[:, tree * width : (tree + 1) * width],
+                    preferred_element_type=jnp.float32,
+                ).astype(jnp.bfloat16)
+                for side in range(2):
+                    block = base + side
+                    held[tree, block] = product[side * rows_owned : (side + 1) * rows_owned]
+                    direction = TREES[tree][0]
+
+                    @pl.when(bits_of(block)[direction] != my_bits[direction])
+                    def _(tree=tree, block=block):
+                        tree_message(tree, 0, block)[0].start()
+
+        for step in range(4):
+            slot = turn - LAG * (step + 1)
+
+            @pl.when(jnp.logical_and(slot >= 0, slot < 8))
+            def _(step=step, slot=slot):
+                base = first_block(slot)
+                for side in range(2):
+                    block = base + side
+                    theirs = bits_of(block)
+                    for tree in range(4):
+                        order = TREES[tree]
+                        same = all_of([theirs[d] == my_bits[d] for d in order[: step + 1]])
+
+                        @pl.when(same)
+                        def _(tree=tree, block=block, order=order, theirs=theirs):
+                            message, index = tree_message(tree, step, block)
+                            message.wait_recv()
+                            total = held[tree, block].astype(jnp.float32) + inbox[tree, index].astype(jnp.float32)
+                            if step == 3:
+                                mixed[:, tree * width : (tree + 1) * width] = total.astype(jnp.bfloat16)
+                            else:
+                                held[tree, block] = total.astype(jnp.bfloat16)
+                                onward = order[step + 1]
+
+                                @pl.when(theirs[onward] != my_bits[onward])
+                                def _():
+                                    tree_message(tree, step + 1, block)[0].start()
+
+        return carry
+
+    lax.fori_loop(0, 8 + 4 * LAG, iteration, 0)
+
+    own_parcel.wait()
+    for step in range(1, 8):
+        source = (row + 8 - step) % 8
+        remote(
+            parcels.at[source], arrived.at[source], parcel_send.at[step], parcel_recv.at[source],
+            {"row": source, "mp": mp},
+        ).wait_recv()
+    rows = jnp.concatenate([arrived[block] for block in range(8)], 0)
+    slots = lax.broadcasted_iota(jnp.int32, (64, 64), 1).astype(jnp.float32)
+    placer = (rows[:, 640:704].astype(jnp.float32) == slots).astype(jnp.bfloat16)
+    placed = lax.dot_general(
+        placer, rows[:, :640], (((0,), (0,)), ((), ())), preferred_element_type=jnp.float32
+    ).astype(jnp.bfloat16)
+    for draft in range(5):
+        next_kv[draft] = placed[:, draft * 128 : (draft + 1) * 128]
+
+    for copy in (to_left, to_right, to_sibling, pass_left, pass_right, share_right, share_left, share_far):
+        copy.wait_send()
+    for step in range(1, 8):
+        target = (row + step) % 8
+        remote(
+            parcels.at[target], arrived.at[row], parcel_send.at[step], parcel_recv.at[row],
+            {"row": target, "mp": mp},
+        ).wait_send()
+
+    def settle(block, carry):
+        @pl.when(block != mp)
+        def _():
+            for tree in range(4):
+                remote(
+                    held.at[tree, block], inbox.at[tree, 0], tree_send.at[tree, block], tree_recv.at[tree, 0],
+                    {"row": row, "mp": along(mp, 0)},
+                ).wait_send()
+
+        return carry
+
+    lax.fori_loop(0, 16, settle, 0)
+
+
+def project(attention, weight, fresh, keyed):
+    tokens, depth = attention.shape
+    columns = weight.shape[1]
+    rows_owned = tokens // 2
+    width = columns // 4
+    bf16 = jnp.bfloat16
+    dma = pltpu.SemaphoreType.DMA
+    return pl.pallas_call(
+        project_kernel,
+        out_shape=(
+            jax.ShapeDtypeStruct((rows_owned, columns), bf16),
+            jax.ShapeDtypeStruct((5, 64, 128), bf16),
+        ),
+        in_specs=[
+            pl.BlockSpec(memory_space=pl.ANY),
+            pl.BlockSpec(memory_space=pl.ANY),
+            pl.BlockSpec(memory_space=pltpu.VMEM),
+            pl.BlockSpec(memory_space=pltpu.VMEM),
+        ],
+        out_specs=(pl.BlockSpec(memory_space=pltpu.VMEM), pl.BlockSpec(memory_space=pltpu.VMEM)),
+        scratch_shapes=[
+            pltpu.VMEM((8, tokens, depth), bf16),
+            pltpu.VMEM((depth, columns), bf16),
+            pltpu.VMEM((4, 16, rows_owned, width), bf16),
+            pltpu.VMEM((4, 15, rows_owned, width), bf16),
+            pltpu.VMEM((8, 8, 768), bf16),
+            pltpu.VMEM((8, 8, 768), bf16),
+            dma((3,)), dma((3,)), dma((5,)), dma((9,)), dma((4, 16)), dma((4, 15)), dma((8,)), dma((8,)),
+        ],
+        compiler_params=pltpu.CompilerParams(
+            collective_id=0, has_side_effects=True, vmem_limit_bytes=56 * 1024 * 1024
+        ),
+        name="project",
+    )(attention, weight, fresh, keyed)
 
 
 def partner(block, axis, bit):
@@ -20,14 +309,31 @@
     return lax.dynamic_slice_in_dim(values, start, count, 3)
 
 
-def shards(queries, new_kv, cache_keys, cache_values, cache_lens, accepted, dest, out_weight):
+def parcel_keys(accepted, dest):
+    target = dest // 64
+    landing = dest % 64
+    beam_index = jnp.arange(64, dtype=jnp.int32)
+    earlier = (target[None, :] == target[:, None]) & (beam_index[None, :] < beam_index[:, None])
+    position = jnp.sum(earlier.astype(jnp.int32), 1)
+    send_slot = target * 8 + position
+    order = jnp.arange(8, dtype=jnp.int32)
+    draft = jnp.arange(5, dtype=jnp.int32)
+    shape = (8, 64, 5)
+    slot = jnp.broadcast_to(send_slot[None, :, None], shape)
+    on = (order[:, None, None] == draft[None, None, :]) & (draft[None, None, :] < accepted[None, :, None])
+    first = (order[:, None, None] == 5) & (draft[None, None, :] == 0)
+    keys = jnp.where(on | first, slot, -1)
+    keys = jnp.where(order[:, None, None] == 6, landing[None, :, None], keys)
+    return keys.reshape(8, 320)
+
+
+def attend(queries, new_kv, cache_keys, cache_values, cache_lens):
     beams_here = cache_keys.shape[0]
     halves_held = cache_keys.shape[1]
     half_length = cache_keys.shape[2]
     head_size = cache_keys.shape[3]
     drafts = queries.shape[0] // beams_here
     heads_owned = queries.shape[1] // head_size
-    kv_columns = new_kv.shape[1]
     mp_place = lax.axis_index("mp")
     lower_side = mp_place % 2 == 0
     partner_queries, partner_fresh = partner((queries, new_kv), "mp", 0)
@@ -96,68 +402,24 @@
     own_partial = head_slice(partial_value, own_start, heads_owned)
     own_highest = head_slice(highest, own_start, heads_owned)
     own_mass = head_slice(weight_mass, own_start, heads_owned)
-    partial_value = jnp.where(
-        lower_side,
-        jnp.concatenate([own_partial, got_partial], 1),
-        jnp.concatenate([got_partial, own_partial], 1),
-    )
-    highest = jnp.where(
-        lower_side,
-        jnp.concatenate([own_highest, got_highest], 1),
-        jnp.concatenate([got_highest, own_highest], 1),
-    )
-    weight_mass = jnp.where(
-        lower_side,
-        jnp.concatenate([own_mass, got_mass], 1),
-        jnp.concatenate([got_mass, own_mass], 1),
-    )
+    partial_value = jnp.concatenate([own_partial, got_partial], 1)
+    highest = jnp.concatenate([own_highest, got_highest], 1)
+    weight_mass = jnp.concatenate([own_mass, got_mass], 1)
     summit = jnp.max(highest, 1)
     factor = jnp.exp(highest - summit[:, None])
     numer = jnp.sum(factor[..., None] * partial_value, 1)
     denom = jnp.sum(factor * weight_mass, 1)
-    attention = (
+    return (
         (numer / denom[..., None])
         .astype(jnp.bfloat16)
         .reshape(beams_here * drafts, heads_owned * head_size)
     )
-    projected = jnp.dot(
-        lax.all_gather(attention, "row", axis=0, tiled=True),
-        out_weight,
-        preferred_element_type=jnp.float32,
-    )
-    rows_owned = projected.shape[0] // lax.axis_size("mp")
-    totals = lax.psum(projected.astype(jnp.bfloat16), "mp").astype(jnp.float32)
-    owned_rows = lax.dynamic_slice_in_dim(totals, mp_place * rows_owned, rows_owned, 0)
-    mixed = owned_rows.astype(jnp.bfloat16)
-    fresh_rows = new_kv.reshape(beams_here, drafts, kv_columns)
-    kept_mask = order[None, :] < accepted[:, None]
-    kept_rows = jnp.where(kept_mask[..., None], fresh_rows, jnp.zeros_like(fresh_rows)).reshape(
-        beams_here, drafts * kv_columns
-    )
-    blocks = lax.axis_size("row")
-    share_count = beams_here // blocks
-    target = dest // beams_here
-    landing = dest % beams_here
-    beam_index = jnp.arange(beams_here, dtype=jnp.int32)
-    earlier = (target[None, :] == target[:, None]) & (beam_index[None, :] < beam_index[:, None])
-    position = jnp.sum(earlier.astype(jnp.int32), 1)
-    send_slot = target * share_count + position
-    picker = send_slot[None, :] == beam_index[:, None]
-    outgoing = jnp.dot(
-        picker.astype(jnp.bfloat16), kept_rows, preferred_element_type=jnp.float32
-    ).astype(jnp.bfloat16)
-    outgoing = outgoing.reshape(blocks, share_count, drafts * kv_columns)
-    labels = jnp.sum(jnp.where(picker, landing[None, :], 0), 1).reshape(blocks, share_count)
-    arrived, arrived_labels = (
-        lax.all_to_all(outgoing, "row", split_axis=0, concat_axis=0, tiled=True),
-        lax.all_to_all(labels, "row", split_axis=0, concat_axis=0, tiled=True),
-    )
-    arrived = arrived.reshape(beams_here, drafts * kv_columns)
-    arrived_labels = arrived_labels.reshape(beams_here)
-    placer = (arrived_labels[None, :] == beam_index[:, None]).astype(jnp.bfloat16)
-    next_kv = jnp.dot(placer, arrived, preferred_element_type=jnp.float32).astype(jnp.bfloat16)
-    next_kv = next_kv.reshape(beams_here, drafts, kv_columns)
-    return (mixed, next_kv)
+
+
+def shards(queries, new_kv, cache_keys, cache_values, cache_lens, accepted, dest, out_weight):
+    attention = attend(queries, new_kv, cache_keys, cache_values, cache_lens)
+    mixed, moved = project(attention, out_weight, new_kv, parcel_keys(accepted, dest))
+    return mixed, moved.transpose(1, 0, 2)
 
 
 def solution(mesh):

time: 308 us -> 175 us (0.57)
  waiting for transfers between devices: 217 us -> 30.7 us
  Pallas kernels: 0 us -> 90.5 us
  matrix products: 34.4 us -> 17 us
  between operations: 14.3 us -> 0.92 us
  starting transfers between devices: 17.2 us -> 6.05 us
  local copies, waits for them, and re-layouts: 6.79 us -> 10.5 us
    psum x1 -> x0, waiting for transfers between devices: 141 us -> none  [shards(): totals = lax.psum(projected.astype(jnp.bfloat16), 'mp').astype(jnp.float32)]
    pallas_call x0 -> x1, Pallas kernels: none -> 90.5 us  [project(): pl.pallas_call(project_kernel, out_shape=(jax.ShapeDtypeStruct((rows_owne...]
    all_gather x1 -> x0, waiting for transfers between devices: 36.4 us -> none  [shards(): lax.all_gather(attention, 'row', axis=0, tiled=True)]
    dot_general x7 -> x4, matrix products: 34.4 us -> 17 us  [the longest x1 6.47 us: attend(): jnp.einsum('btjd,bsid->bstji', query_block, cache_keys, preferred_element...]
    all_to_all x2 -> x0, starting transfers between devices: 11 us -> none  [the longest x1 5.63 us: shards(): lax.all_to_all(labels, 'row', split_axis=0, concat_axis=0, tiled=True)]
    all_to_all x2 -> x0, waiting for transfers between devices: 4.33 us -> none  [the longest x1 2.36 us: shards(): lax.all_to_all(outgoing, 'row', split_axis=0, concat_axis=0, tiled=True)]
    ppermute x5, waiting for transfers between devices: 34.5 us -> 30.7 us  [partner(): return lax.ppermute(block, axis, route)]
    unnamed x12, local copies, waits for them, and re-layouts: 1.9 us -> 5.54 us
  transfers between devices with their start and end apart: 9 -> 5, of which waited for: 7 -> 2; matrix products, arithmetic and copies ran while one was open for 5% -> 8% of each run, Pallas kernels for 0% -> 0%
where the time goes in v1:
time: 175 us; the launch traced here: 173 us
  Pallas kernels  90.5 us (52%)
  waiting for transfers between devices  30.7 us (18%)
  other arithmetic  17.1 us (10%)
  matrix products  17 us (10%)
  local copies, waits for them, and re-layouts  10.5 us (6%)
  starting transfers between devices  6.05 us (3%)
    pallas_call x1, Pallas kernels, project(): pl.pallas_call(project_kernel, out_shape=(jax.ShapeDtypeStruct((rows_owne...  90.5 us
    ppermute x5, waiting for transfers between devices, partner(): return lax.ppermute(block, axis, route)  30.7 us
    reduce_sum x1, other arithmetic, attend(): jnp.sum(cache_weights.astype(jnp.float32), -1)  6.68 us
    dot_general x1, matrix products, attend(): jnp.einsum('btjd,bsid->bstji', query_block, cache_keys, preferred_element...  6.47 us
    ppermute x5, starting transfers between devices, partner(): return lax.ppermute(block, axis, route)  6.05 us
    dot_general x1, matrix products, attend(): jnp.einsum('bstji,bsid->bstjd', cache_weights, cache_values, preferred_el...  5.68 us
    unnamed x12, local copies, waits for them, and re-layouts  5.54 us
  transfers between devices with their start and end apart: 5, of which 2 were waited for; matrix products, arithmetic and copies ran while one was open for 8% of the time, Pallas kernels for 0%

profile of v1, /device:TPU:14, one launch (start us, length us, event | category | flops | bytes accessed | tf_op | source)
XLA Modules:
  0.0 172.8 jit_solution(1089721107108187190)
XLA Ops:
  0.6 2.0 %collective-permute-start.1 = (bf16[320,128]{1,0:T(8,128)(2,1)}, bf16[320,128]{1,0:T(8,128)(2,1)S(1)}, u32[]{:S(2)}, u32[]{:S(2)}) collective-permute-start(bf16[320,128]{1,0:T(8,128)(2,1)} %fresh.1), channel_id=1, source_target_pairs={{0,1},{1,0},{2,3},{3,2},{4,5},{5,4},{6,7},{7,6},{8,9},{9,8},{10,11... | collective-permute-start | bytes 245768 | tf_op jit(solution)/shard_map/ppermute | solution.py:305
  2.6 0.1 collective-permute-start
  2.8 0.7 and_select_fusion.1
  3.4 0.2 convert_reduce_fusion.2
  3.6 0.8 fusion.13
  4.4 0.7 broadcast_compare_fusion
  5.2 0.1 broadcast_in_dim.114
  5.2 0.1 broadcast_in_dim.115
  5.4 0.1 broadcast_in_dim.111
  5.4 0.1 broadcast_in_dim.112
  5.6 0.7 lt.89
  6.3 0.1 lt.90
  6.5 0.1 lt.88
  6.6 0.2 and.98
  6.8 0.1 broadcast_and_fusion.1
  7.0 0.2 or.12
  7.2 0.7 select_select_fusion.keyed
  7.9 0.0 collective-permute-done.1
  7.9 1.0 maximum_select_fusion.1
  9.0 0.2 fusion.18
  9.2 10.2 %collective-permute-done = bf16[320,1024]{1,0:T(8,128)(2,1)S(1)} collective-permute-done((bf16[320,1024]{1,0:T(8,128)(2,1)}, bf16[320,1024]{1,0:T(8,128)(2,1)S(1)}, u32[]{:S(2)}, u32[]{:S(2)}) %collective-permute-start) | collective-permute-done | bytes 655392 | tf_op jit(solution)/shard_map/ppermute | solution.py:305
  19.4 1.8 %fusion.9 = bf16[40,8,16,128]{3,1,2,0:T(8,128)(2,1)S(1)} fusion(bf16[320,1024]{1,0:T(8,128)(2,1)S(1)} %collective-permute-done, bf16[320,1024]{1,0:T(8,128)(2,1)} %param.8, pred[]{:T(512)S(6)} %eq.79), kind=kLoop, calls=%fused_computation.16 | loop fusion | flops 5898240 | bytes 2621441
  21.2 0.3 copy.45
  21.5 3.2 %fusion.19 = (f32[64,5,16]{2,1,0:T(8,128)S(1)}, f32[64,5,16,5]{2,3,1,0:T(8,128)S(1)}) fusion(bf16[64,5,16,128]{3,2,1,0:T(8,128)(2,1)S(1)} %bitcast.85, bf16[64,5,1,128]{3,2,1,0:T(2,128)(2,1)S(1)} %get-tuple-element.15, pred[64,5,5]{2,1,0:T(8,128)(4,1)S(1)} %broadcast_and_fusion), kind=kOutput, calls=%fused_computation.65 | convolution fusion | flops 6625280 | bytes 1517120 | tf_op jit(solution)/shard_map/btjd,bud->btju/dot_general | solution.py:362
  24.6 6.5 %fusion.1 = (f32[64,5,16]{2,1,0:T(8,128)S(1)}, f32[64,5,16,512]{3,2,1,0:T(8,128)S(1)}) fusion(pred[64,512]{1,0:T(8,128)(4,1)S(1)} %broadcast_compare_fusion, bf16[64,5,16,128]{3,2,1,0:T(8,128)(2,1)S(1)} %bitcast.86, bf16[64,1,512,128]{3,2,1,0:T(8,128)(2,1)} %param.10), kind=kOutput, calls=%fused_computation.4 | convolution fusion | flops 678947840 | bytes 20238336 | tf_op jit(solution)/shard_map/btjd,bsid->bstji/dot_general | solution.py:358
  31.1 0.0 copy-start
  31.2 2.0 %convert_reduce_fusion.1 = f32[64,5,16]{2,1,0:T(8,128)} fusion(f32[64,5,16,5]{2,3,1,0:T(8,128)S(1)} %get-tuple-element.21, f32[64,5,16]{2,1,0:T(8,128)S(1)} %max.16, pred[64,5,5]{2,1,0:T(8,128)(4,1)S(1)} %broadcast_and_fusion), kind=kLoop, calls=%fused_computation.18 | loop fusion | flops 122880 | bytes 144960 | tf_op jit(solution)/shard_map/reduce_sum | solution.py:388
  33.1 1.6 constant_dynamic-slice_fusion.3
  34.7 5.7 %fusion.2 = f32[64,5,16,128]{3,2,1,0:T(8,128)S(1)} fusion(bf16[64,1,512,128]{3,2,1,0:T(8,128)(2,1)} %param.11, f32[64,5,16,512]{3,2,1,0:T(8,128)S(1)} %get-tuple-element.19, f32[64,5,16]{2,1,0:T(8,128)S(1)} %max.16, pred[64,512]{1,0:T(8,128)(4,1)S(1)} %broadcast_compare_fusion), kind=kOutput, calls=%fused_computation.5 | convolution fusion | flops 684195840 | bytes 21549056 | tf_op jit(solution)/shard_map/bstji,bsid->bstjd/dot_general | solution.py:382
  40.4 0.0 copy-done
  40.4 1.7 convolution_add_fusion
  42.1 0.0 copy-start.2
  42.1 0.2 dynamic-slice_bitcast_fusion.1
  42.3 0.8 copy-done.2
  43.1 0.1 copy.33
  43.2 1.7 collective-permute-start.2
  44.9 0.0 copy-start.3
  44.9 0.0 copy-start.1
  44.9 0.4 collective-permute-start.3
  45.3 6.7 %convert_reduce_fusion = f32[64,5,16]{2,1,0:T(8,128)S(1)} fusion(f32[64,5,16]{2,1,0:T(8,128)S(1)} %max.16, f32[64,5,16,512]{3,2,1,0:T(8,128)} %copy-done, pred[64,512]{1,0:T(8,128)(4,1)S(1)} %broadcast_compare_fusion), kind=kLoop, calls=%fused_computation.2 | loop fusion | flops 18344960 | bytes 10559488 | tf_op jit(solution)/shard_map/reduce_sum | solution.py:388
  51.9 0.0 copy-done.3
  52.0 0.2 constant_dynamic-slice_fusion.1
  52.2 0.1 copy.36
  52.3 0.1 copy.37
  52.4 1.9 %collective-permute-start.4 = (f32[64,1,5,8]{0,3,2,1:T(8,128)S(1)}, f32[64,1,5,8]{0,3,2,1:T(8,128)S(1)}, u32[]{:S(2)}, u32[]{:S(2)}) collective-permute-start(f32[64,1,5,8]{0,3,2,1:T(8,128)S(1)} %bitcast.93), channel_id=1, source_target_pairs={{0,1},{1,0},{2,3},{3,2},{4,5},{5,4},{6,7},{7,6},{8,9},{9,8},{10,11... | collective-permute-start | bytes 30728 | tf_op jit(solution)/shard_map/ppermute | solution.py:305
  54.3 0.0 copy-done.1
  54.3 0.1 copy.32
  54.4 0.0 collective-permute-done.2
  54.4 20.5 %collective-permute-done.4 = f32[64,1,5,8]{0,3,2,1:T(8,128)S(1)} collective-permute-done((f32[64,1,5,8]{0,3,2,1:T(8,128)S(1)}, f32[64,1,5,8]{0,3,2,1:T(8,128)S(1)}, u32[]{:S(2)}, u32[]{:S(2)}) %collective-permute-start.4) | collective-permute-done | bytes 10272 | tf_op jit(solution)/shard_map/ppermute | solution.py:305
  74.9 0.1 copy.38
  75.1 0.2 copy.34
  75.3 0.0 collective-permute-done.3
  75.4 2.0 %fusion.7 = f32[64,5,8,128]{3,2,1,0:T(8,128)S(1)} fusion(f32[64,1,5,8,128]{4,3,2,0,1:T(8,128)} %collective-permute-done.3, f32[64,1,5,8,128]{4,3,2,0,1:T(8,128)S(1)} %get-tuple-element.8, f32[64,2,5,8]{3,2,0,1:T(8,128)S(1)} %copy.34), kind=kLoop, calls=%fused_computation.11 | loop fusion | flops 1638400 | bytes 3952640 | tf_op jit(solution)/shard_map/reduce_sum | solution.py:410
  77.4 0.4 divide_convert_fusion
  77.8 1.0 copy.54
  78.8 90.5 %project.1 = (bf16[160,2048]{1,0:T(8,128)(2,1)}, bf16[5,64,128]{2,1,0:T(8,128)(2,1)}) custom-call(bf16[320,1024]{1,0:T(8,128)(2,1)} %bitcast.88, bf16[1024,2048]{1,0:T(8,128)(2,1)} %weight.1, bf16[320,128]{1,0:T(8,128)(2,1)} %fresh.1, s32[8,320]{1,0:T(8,128)} %select_select_fusion.keyed), custom_call_target="tpu_custom_call" | custom-call | tf_op jit(solution)/shard_map/project/pallas_call | solution.py:269
  169.3 2.0 %copy.57 = bf16[160,2048]{1,0:T(8,128)(2,1)} copy(bf16[160,2048]{1,0:T(8,128)(2,1)} %get-tuple-element.24) | data formatting | bytes 1310720
  171.3 1.5 copy.58
  (17 shorter events, 0.3 us)
Async XLA Ops:
  0.6 7.3 %collective-permute-start.1 = (bf16[320,128]{1,0:T(8,128)(2,1)}, bf16[320,128]{1,0:T(8,128)(2,1)S(1)}, u32[]{:S(2)}, u32[]{:S(2)}) collective-permute-start(bf16[320,128]{1,0:T(8,128)(2,1)} %fresh.1), channel_id=1, source_target_pairs={{0,1},{1,0},{2,3},{3,2},{4,5},{5,4},{6,7},{7,6},{8,9},{9,8},{10,11... | collective-permute-start | bytes 245768 | tf_op jit(solution)/shard_map/ppermute | solution.py:305
  2.6 16.8 %collective-permute-start = (bf16[320,1024]{1,0:T(8,128)(2,1)}, bf16[320,1024]{1,0:T(8,128)(2,1)S(1)}, u32[]{:S(2)}, u32[]{:S(2)}) collective-permute-start(bf16[320,1024]{1,0:T(8,128)(2,1)} %param.8), channel_id=1, source_target_pairs={{0,1},{1,0},{2,3},{3,2},{4,5},{5,4},{6,7},{7,6},{8,9},{9,8},{10,11... | collective-permute-start | bytes 1966088 | tf_op jit(solution)/shard_map/ppermute | solution.py:305
  31.1 9.3 %copy-start = (f32[64,5,16,512]{3,2,1,0:T(8,128)}, f32[64,5,16,512]{3,2,1,0:T(8,128)S(1)}, u32[]{:S(2)}) copy-start(f32[64,5,16,512]{3,2,1,0:T(8,128)S(1)} %get-tuple-element.19) | copy-start | bytes 31457284
  42.1 1.0 copy-start.2
  43.2 11.2 %collective-permute-start.2 = (f32[64,1,5,8]{0,3,2,1:T(8,128)S(1)}, f32[64,1,5,8]{0,3,2,1:T(8,128)S(1)}, u32[]{:S(2)}, u32[]{:S(2)}) collective-permute-start(f32[64,1,5,8]{0,3,2,1:T(8,128)S(1)} %bitcast.92), channel_id=1, source_target_pairs={{0,1},{1,0},{2,3},{3,2},{4,5},{5,4},{6,7},{7,6},{8,9},{9,8},{10,11... | collective-permute-start | bytes 30728 | tf_op jit(solution)/shard_map/ppermute | solution.py:305
  44.9 7.1 %copy-start.3 = (f32[64,5,16]{2,1,0:T(8,128)S(1)}, f32[64,5,16]{2,1,0:T(8,128)}, u32[]{:S(2)}) copy-start(f32[64,5,16]{2,1,0:T(8,128)} %convert_reduce_fusion.1) | copy-start | bytes 61444
  44.9 9.4 %copy-start.1 = (f32[64,5,8]{2,1,0:T(8,128)S(1)}, f32[64,5,8]{2,1,0:T(8,128)}, u32[]{:S(2)}) copy-start(f32[64,5,8]{2,1,0:T(8,128)} %get-tuple-element.10) | copy-start | bytes 30724
  44.9 30.4 %collective-permute-start.3 = (f32[64,1,5,8,128]{4,3,2,0,1:T(8,128)S(1)}, f32[64,1,5,8,128]{4,3,2,0,1:T(8,128)}, u32[]{:S(2)}, u32[]{:S(2)}) collective-permute-start(f32[64,1,5,8,128]{4,3,2,0,1:T(8,128)S(1)} %get-tuple-element.9), channel_id=1, source_target_pairs={{0,1},{1,0},{2,3},{3,2},{4,5},{5,4},{6,7},{7,6},{8,9},{9,8},{10,11... | collective-permute-start | bytes 3932168 | tf_op jit(solution)/shard_map/ppermute | solution.py:305
  52.4 22.5 %collective-permute-start.4 = (f32[64,1,5,8]{0,3,2,1:T(8,128)S(1)}, f32[64,1,5,8]{0,3,2,1:T(8,128)S(1)}, u32[]{:S(2)}, u32[]{:S(2)}) collective-permute-start(f32[64,1,5,8]{0,3,2,1:T(8,128)S(1)} %bitcast.93), channel_id=1, source_target_pairs={{0,1},{1,0},{2,3},{3,2},{4,5},{5,4},{6,7},{7,6},{8,9},{9,8},{10,11... | collective-permute-start | bytes 30728 | tf_op jit(solution)/shard_map/ppermute | solution.py:305

commit v2 on v1

v2 whole, which is shorter than its diff:
```python
import functools

import jax
import jax.numpy as jnp
from jax import lax
from jax.experimental import pallas as pl
from jax.experimental.pallas import tpu as pltpu
from jax.sharding import PartitionSpec as P

MESH = pl.DeviceIdType.MESH
masked_score = -1e30

TREES = ((0, 2, 1, 3), (2, 1, 3, 0), (1, 3, 0, 2), (3, 0, 2, 1))
STEP_BASE = (0, 8, 12, 14)
LAG = 2


def bits_of(place):
    y, z = place // 4, place % 4
    return (((y + 1) // 2) % 2, y // 2, ((z + 1) // 2) % 2, z // 2)


def along(place, direction):
    y, z = place // 4, place % 4
    if direction == 0:
        y = y + 1 - 2 * (y % 2)
    elif direction == 1:
        y = 3 - y
    elif direction == 2:
        z = z + 1 - 2 * (z % 2)
    else:
        z = 3 - z
    return y * 4 + z


def all_of(terms):
    result = terms[0]
    for term in terms[1:]:
        result = jnp.logical_and(result, term)
    return result

LOG2E = 1.4426950408889634
CHUNKS = 4
UNROLL = 4


def remote(source, target, send_sem, recv_sem, device):
    return pltpu.make_async_remote_copy(
        src_ref=source, dst_ref=target, send_sem=send_sem, recv_sem=recv_sem,
        device_id=device, device_id_type=MESH,
    )


def dot_nt(left, right):
    return lax.dot_general(
        left, right, (((1,), (1,)), ((), ())), preferred_element_type=jnp.float32
    )


def exchange_and_attend(
    lens, queries, fresh, keys, values, side, pair, publish, forward,
    query_rows, query_out, query_in, fresh_in, key_slots, value_slots,
    sum_own, top_own, mass_own, sum_fresh, top_fresh, mass_fresh, part_out, part_in, stat_out, stat_in,
    cache_sem, fresh_sem, query_send, query_recv, part_send, part_recv, stat_send, stat_recv,
):
    beams = keys.shape[0]
    per = beams // CHUNKS
    tokens = per * 5
    span = keys.shape[1]
    scale = 128 ** -0.5 * LOG2E

    def cache_copies(chunk, slot):
        return (
            pltpu.make_async_copy(keys.at[pl.ds(chunk * per, per)], key_slots.at[slot], cache_sem.at[0, slot]),
            pltpu.make_async_copy(values.at[pl.ds(chunk * per, per)], value_slots.at[slot], cache_sem.at[1, slot]),
        )

    def query_message(chunk):
        return remote(query_out.at[chunk], query_in.at[chunk], query_send.at[chunk], query_recv.at[chunk], pair)

    def part_message(chunk):
        return remote(part_out.at[chunk], part_in.at[chunk], part_send.at[chunk], part_recv.at[chunk], pair)

    def stat_message(chunk):
        return remote(stat_out.at[chunk], stat_in.at[chunk], stat_send.at[chunk], stat_recv.at[chunk], pair)

    fresh_message = remote(fresh, fresh_in, fresh_sem.at[0], fresh_sem.at[1], pair)

    def send_query(chunk, carry):
        for head in range(8):
            query_rows[chunk, pl.ds(head, tokens, stride=8), :] = queries[
                pl.ds(chunk * tokens, tokens), head * 128 : (head + 1) * 128
            ].astype(jnp.float32)
        for part in range(per):
            query_out[chunk, part] = query_rows[chunk, part * 40 : part * 40 + 40, :].astype(jnp.bfloat16)
        query_message(chunk).start()

        @pl.when(chunk == 0)
        def _():
            fresh_message.start()

        return carry

    lax.fori_loop(0, CHUNKS, send_query, 0)
    fresh_message.wait_recv()

    rows = per * 40
    row_of = lax.broadcasted_iota(jnp.int32, (rows, tokens), 0)
    key_of = lax.broadcasted_iota(jnp.int32, (rows, tokens), 1)
    fresh_valid = jnp.logical_and(
        row_of // 40 == key_of // 5, (row_of % 40) // 8 >= key_of % 5
    )
    lane = lax.broadcasted_iota(jnp.int32, (40, 128), 1)
    spot = lax.broadcasted_iota(jnp.int32, (80, span), 1) + side * span
    even = side == 0

    def attend_chunk(chunk, carry):
        slot = chunk % 2
        for copy in cache_copies(chunk, slot):
            copy.wait()

        @pl.when(chunk + 1 < CHUNKS)
        def _():
            for copy in cache_copies(chunk + 1, 1 - slot):
                copy.start()

        mine = fresh[pl.ds(chunk * tokens, tokens), :]
        theirs = fresh_in[pl.ds(chunk * tokens, tokens), :]
        fresh_keys = jnp.where(even, mine, theirs)
        fresh_values = jnp.where(even, theirs, mine)
        scores = dot_nt(query_rows[chunk].astype(jnp.bfloat16), fresh_keys)
        scores = jnp.where(fresh_valid, scores, masked_score)
        highest = jnp.max(scores, 1, keepdims=True)
        weights = jnp.exp2((scores - highest) * scale).astype(jnp.bfloat16)
        sums = jnp.dot(
            weights, jnp.concatenate([fresh_values, jnp.ones_like(fresh_values)], 1),
            preferred_element_type=jnp.float32,
        )
        sum_fresh[...] = sums[:, :128]
        mass_fresh[...] = sums[:, 128:]
        top_fresh[...] = jnp.broadcast_to(highest * scale, (rows, 128))

        query_message(chunk).wait_recv()

        def beams_step(group, stat):
            for member in range(UNROLL):
                local = group * UNROLL + member
                at = pl.multiple_of(local * 40, 8)
                block = jnp.concatenate(
                    [
                        query_rows[chunk, pl.ds(at, 40), :],
                        query_in[chunk, local].astype(jnp.float32),
                    ],
                    0,
                ).astype(jnp.bfloat16)
                scores = dot_nt(block, key_slots[slot, local])
                scores = jnp.where(spot < lens[chunk * per + local], scores, masked_score)
                highest = jnp.max(scores, 1, keepdims=True)
                weights = jnp.exp2((scores - highest) * scale).astype(jnp.bfloat16)
                value = value_slots[slot, local]
                sums = jnp.dot(
                    weights, jnp.concatenate([value, jnp.ones_like(value)], 1),
                    preferred_element_type=jnp.float32,
                )
                top = jnp.broadcast_to(highest * scale, (80, 128))
                part_out[chunk, local] = (sums[40:, :128] / sums[40:, 128:]).astype(jnp.bfloat16)
                stat = jnp.where(lane == local, top[40:] + jnp.log2(sums[40:, 128:]), stat)
                near = top_fresh[pl.ds(at, 40), :]
                summit = jnp.maximum(top[:40], near)
                here = jnp.exp2(top[:40] - summit)
                there = jnp.exp2(near - summit)
                sum_own[chunk, pl.ds(at, 40), :] = sums[:40, :128] * here + sum_fresh[pl.ds(at, 40), :] * there
                mass_own[chunk, pl.ds(at, 40), :] = sums[:40, 128:] * here + mass_fresh[pl.ds(at, 40), :] * there
                top_own[chunk, pl.ds(at, 40), :] = summit
            return stat

        stat_out[chunk] = lax.fori_loop(0, per // UNROLL, beams_step, jnp.zeros((40, 128), jnp.float32))
        part_message(chunk).start()
        stat_message(chunk).start()
        return carry

    lax.fori_loop(0, CHUNKS, attend_chunk, 0)

    def combine_chunk(chunk, carry):
        part_message(chunk).wait_recv()
        stat_message(chunk).wait_recv()

        def beams_step(group, inner):
            stat = stat_in[chunk]
            for member in range(UNROLL):
                local = group * UNROLL + member
                at = pl.multiple_of(local * 40, 8)
                other = jnp.sum(jnp.where(lane == local, stat, 0.0), 1, keepdims=True)
                top = top_own[chunk, pl.ds(at, 40), :]
                summit = jnp.maximum(top, other)
                here = jnp.exp2(top - summit)
                there = jnp.exp2(other - summit)
                total = sum_own[chunk, pl.ds(at, 40), :] * here + part_in[chunk, local].astype(jnp.float32) * there
                mass = mass_own[chunk, pl.ds(at, 40), :] * here + there
                sum_fresh[pl.ds(at, 40), :] = total / mass
            return inner

        lax.fori_loop(0, per // UNROLL, beams_step, 0)
        publish(chunk, sum_fresh)
        forward(chunk)
        return carry

    lax.fori_loop(0, CHUNKS, combine_chunk, 0)

    def settle():
        fresh_message.wait_send()

        def one(chunk, carry):
            query_message(chunk).wait_send()
            part_message(chunk).wait_send()
            stat_message(chunk).wait_send()
            return carry

        lax.fori_loop(0, CHUNKS, one, 0)

    return settle


def attention_scratch(beams, span):
    per = beams // CHUNKS
    bf16, f32 = jnp.bfloat16, jnp.float32
    dma = pltpu.SemaphoreType.DMA
    return [
        pltpu.VMEM((CHUNKS, per * 40, 128), f32),
        pltpu.VMEM((CHUNKS, per, 40, 128), bf16),
        pltpu.VMEM((CHUNKS, per, 40, 128), bf16),
        pltpu.VMEM((beams * 5, 128), bf16),
        pltpu.VMEM((2, per, span, 128), bf16),
        pltpu.VMEM((2, per, span, 128), bf16),
        pltpu.VMEM((CHUNKS, per * 40, 128), f32),
        pltpu.VMEM((CHUNKS, per * 40, 128), f32),
        pltpu.VMEM((CHUNKS, per * 40, 128), f32),
        pltpu.VMEM((per * 40, 128), f32),
        pltpu.VMEM((per * 40, 128), f32),
        pltpu.VMEM((per * 40, 128), f32),
        pltpu.VMEM((CHUNKS, per, 40, 128), bf16),
        pltpu.VMEM((CHUNKS, per, 40, 128), bf16),
        pltpu.VMEM((CHUNKS, 40, 128), f32),
        pltpu.VMEM((CHUNKS, 40, 128), f32),
        dma((2, 2)), dma((2,)), dma((CHUNKS,)), dma((CHUNKS,)), dma((CHUNKS,)), dma((CHUNKS,)), dma((CHUNKS,)), dma((CHUNKS,)),
    ]


GATHER_KINDS = (
    "to_right", "to_left", "to_sibling", "share_right", "share_left", "share_far", "pass_left", "pass_right",
)


def step_kernel(
    lens, queries, keys, values, weight, fresh, keyed, mixed, next_kv,
    gathered, weight_here, held, inbox, parcels, arrived,
    local_sem, own_send, far_send, gather_recv, tree_send, tree_recv, parcel_send, parcel_recv, *attention_refs,
):
    row, mp = lax.axis_index("row"), lax.axis_index("mp")
    x, core = row // 2, row % 2
    sibling = {"row": x * 2 + 1 - core, "mp": mp}
    right = {"row": ((x + 1) % 4) * 2 + core, "mp": mp}
    left = {"row": ((x + 3) % 4) * 2 + core, "mp": mp}
    pair = {"row": row, "mp": along(mp, 2)}
    key_slots, value_slots, cache_sem = attention_refs[4], attention_refs[5], attention_refs[16]
    per = keys.shape[0] // CHUNKS
    pltpu.make_async_copy(keys.at[pl.ds(0, per)], key_slots.at[0], cache_sem.at[0, 0]).start()
    pltpu.make_async_copy(values.at[pl.ds(0, per)], value_slots.at[0], cache_sem.at[1, 0]).start()
    weight_copy = pltpu.make_async_copy(weight, weight_here, local_sem.at[0])
    weight_copy.start()

    barrier = pltpu.get_barrier_semaphore()
    for step in range(1, 8):
        pl.semaphore_signal(
            barrier, inc=1, device_id={"row": (row + step) % 8, "mp": mp}, device_id_type=MESH
        )
    for direction in range(4):
        pl.semaphore_signal(
            barrier, inc=1, device_id={"row": row, "mp": along(mp, direction)}, device_id_type=MESH
        )
    pl.semaphore_wait(barrier, 11)

    tokens = gathered.shape[1] // CHUNKS
    half = gathered.shape[2] // 2

    def gather_message(kind, chunk):
        at = pl.ds(pl.multiple_of(chunk * tokens, 8), tokens)
        source, target, device = {
            "to_right": (0, 3, right), "to_left": (0, 2, left), "to_sibling": (0, 1, sibling),
            "share_right": (2, 4, sibling), "share_left": (3, 5, sibling), "share_far": (6, 7, sibling),
            "pass_left": (2, 6, left), "pass_right": (3, 6, right),
        }[kind]
        number = GATHER_KINDS.index(kind)
        send, recv = far_send.at[number, chunk], gather_recv.at[number, chunk]
        if kind == "pass_left":
            part = pl.ds(0, half)
            return remote(gathered.at[2, at, part], gathered.at[6, at, part], send, recv, device)
        if kind == "pass_right":
            part = pl.ds(half, half)
            return remote(gathered.at[3, at, part], gathered.at[6, at, part], send, recv, device)
        return remote(gathered.at[source, at], gathered.at[target, at], send, recv, device)

    def publish(chunk, rows):
        at = pl.ds(pl.multiple_of(chunk * tokens, 8), tokens)
        for head in range(8):
            gathered[0, at, head * 128 : (head + 1) * 128] = rows[pl.ds(head, tokens, stride=8), :].astype(
                jnp.bfloat16
            )
        for kind in ("to_right", "to_left", "to_sibling"):
            gather_message(kind, chunk).start()

    def near(chunk):
        gather_message("to_left", chunk).wait_recv()
        gather_message("pass_left", chunk).start()
        gather_message("share_right", chunk).start()
        gather_message("to_right", chunk).wait_recv()
        gather_message("pass_right", chunk).start()
        gather_message("share_left", chunk).start()

    def far(chunk):
        gather_message("pass_left", chunk).wait_recv()
        gather_message("pass_right", chunk).wait_recv()
        gather_message("share_far", chunk).start()

    def forward(chunk):
        @pl.when(chunk >= 1)
        def _():
            near(chunk - 1)

        @pl.when(chunk >= 2)
        def _():
            far(chunk - 2)

    place = lax.broadcasted_iota(jnp.int32, (64, 320), 0)
    fresh_rows = fresh[...]
    columns = []
    for draft in range(5):
        pick = (keyed[draft : draft + 1, :] == place).astype(jnp.bfloat16)
        columns.append(
            jnp.dot(pick, fresh_rows, preferred_element_type=jnp.float32).astype(jnp.bfloat16)
        )
    label = jnp.sum(
        jnp.where(keyed[5:6, :] == place, keyed[6:7, :], 0).astype(jnp.float32), 1, keepdims=True
    )
    columns.append(jnp.broadcast_to(label, (64, 128)).astype(jnp.bfloat16))
    for block in range(8):
        for part, column in enumerate(columns):
            parcels[block, :, pl.ds(part * 128, 128)] = column[block * 8 : block * 8 + 8]
    own_parcel = pltpu.make_async_copy(parcels.at[row], arrived.at[row], local_sem.at[2])
    own_parcel.start()
    for step in range(1, 8):
        target = (row + step) % 8
        remote(
            parcels.at[target], arrived.at[row], parcel_send.at[step], parcel_recv.at[row],
            {"row": target, "mp": mp},
        ).start()

    settle_attention = exchange_and_attend(
        lens, queries, fresh, keys, values, mp % 2, pair, publish, forward, *attention_refs
    )
    near(CHUNKS - 1)
    far(CHUNKS - 2)
    weight_copy.wait()

    rows_owned = mixed.shape[0]
    width = held.shape[3]
    my_bits = bits_of(mp)

    def tree_message(tree, step, block):
        order = TREES[tree]
        rest = bits_of(block)
        index = STEP_BASE[step]
        for power, direction in enumerate(order[step + 1 :]):
            index = index + rest[direction] * (1 << power)
        return remote(
            held.at[tree, block], inbox.at[tree, index], tree_send.at[tree, block],
            tree_recv.at[tree, index], {"row": row, "mp": along(mp, order[step])},
        ), index

    def first_block(slot):
        shift = jnp.where(slot < 2, 0, jnp.where(slot >= 6, 2, jnp.where(slot % 2 == 0, 1, 3)))
        other = jnp.where(slot < 6, jnp.where(slot < 2, slot, jnp.where(slot >= 4, 1, 0)), slot - 6)
        owner = ((x + shift) % 4) * 2 + jnp.where(other == 1, 1 - core, core)
        return owner * 2

    def iteration(turn, carry):
        def arrive(kind):
            def one(chunk, inner):
                gather_message(kind, chunk).wait_recv()
                return inner

            lax.fori_loop(0, CHUNKS, one, 0)

        @pl.when(turn == 1)
        def _():
            arrive("to_sibling")

        @pl.when(turn == 4)
        def _():
            arrive("share_right")

        @pl.when(turn == 5)
        def _():
            far(CHUNKS - 1)
            arrive("share_left")

        @pl.when(turn == 7)
        def _():
            arrive("share_far")

        @pl.when(turn < 8)
        def _():
            base = first_block(turn)
            for tree in range(4):
                product = jnp.dot(
                    gathered[turn], weight_here[:, tree * width : (tree + 1) * width],
                    preferred_element_type=jnp.float32,
                ).astype(jnp.bfloat16)
                for side in range(2):
                    block = base + side
                    held[tree, block] = product[side * rows_owned : (side + 1) * rows_owned]
                    direction = TREES[tree][0]

                    @pl.when(bits_of(block)[direction] != my_bits[direction])
                    def _(tree=tree, block=block):
                        tree_message(tree, 0, block)[0].start()

        for step in range(4):
            slot = turn - LAG * (step + 1)

            @pl.when(jnp.logical_and(slot >= 0, slot < 8))
            def _(step=step, slot=slot):
                base = first_block(slot)
                for side in range(2):
                    block = base + side
                    theirs = bits_of(block)
                    for tree in range(4):
                        order = TREES[tree]
                        same = all_of([theirs[d] == my_bits[d] for d in order[: step + 1]])

                        @pl.when(same)
                        def _(tree=tree, block=block, order=order, theirs=theirs):
                            message, index = tree_message(tree, step, block)
                            message.wait_recv()
                            total = held[tree, block].astype(jnp.float32) + inbox[tree, index].astype(jnp.float32)
                            if step == 3:
                                mixed[:, tree * width : (tree + 1) * width] = total.astype(jnp.bfloat16)
                            else:
                                held[tree, block] = total.astype(jnp.bfloat16)
                                onward = order[step + 1]

                                @pl.when(theirs[onward] != my_bits[onward])
                                def _():
                                    tree_message(tree, step + 1, block)[0].start()

        return carry

    lax.fori_loop(0, 8 + 4 * LAG, iteration, 0)

    own_parcel.wait()
    for step in range(1, 8):
        source = (row + 8 - step) % 8
        remote(
            parcels.at[source], arrived.at[source], parcel_send.at[step], parcel_recv.at[source],
            {"row": source, "mp": mp},
        ).wait_recv()
    rows = jnp.concatenate([arrived[block] for block in range(8)], 0)
    slots = lax.broadcasted_iota(jnp.int32, (64, 64), 1).astype(jnp.float32)
    placer = (rows[:, 640:704].astype(jnp.float32) == slots).astype(jnp.bfloat16)
    placed = lax.dot_general(
        placer, rows[:, :640], (((0,), (0,)), ((), ())), preferred_element_type=jnp.float32
    ).astype(jnp.bfloat16)
    for draft in range(5):
        next_kv[draft] = placed[:, draft * 128 : (draft + 1) * 128]

    def settle_gather(chunk, carry):
        for kind in GATHER_KINDS:
            gather_message(kind, chunk).wait_send()
        return carry

    lax.fori_loop(0, CHUNKS, settle_gather, 0)
    settle_attention()
    for step in range(1, 8):
        target = (row + step) % 8
        remote(
            parcels.at[target], arrived.at[row], parcel_send.at[step], parcel_recv.at[row],
            {"row": target, "mp": mp},
        ).wait_send()

    def settle(block, carry):
        @pl.when(block != mp)
        def _():
            for tree in range(4):
                remote(
                    held.at[tree, block], inbox.at[tree, 0], tree_send.at[tree, block], tree_recv.at[tree, 0],
                    {"row": row, "mp": along(mp, 0)},
                ).wait_send()

        return carry

    lax.fori_loop(0, 16, settle, 0)


def step(lens, queries, keys, values, weight, fresh, keyed):
    tokens, depth = queries.shape
    columns = weight.shape[1]
    rows_owned = tokens // 2
    width = columns // 4
    bf16 = jnp.bfloat16
    dma = pltpu.SemaphoreType.DMA
    vmem = pl.BlockSpec(memory_space=pltpu.VMEM)
    hbm = pl.BlockSpec(memory_space=pl.ANY)
    return pl.pallas_call(
        step_kernel,
        out_shape=(
            jax.ShapeDtypeStruct((rows_owned, columns), bf16),
            jax.ShapeDtypeStruct((5, 64, 128), bf16),
        ),
        in_specs=[pl.BlockSpec(memory_space=pltpu.SMEM), vmem, hbm, hbm, hbm, vmem, vmem],
        out_specs=(vmem, vmem),
        scratch_shapes=[
            pltpu.VMEM((8, tokens, depth), bf16),
            pltpu.VMEM((depth, columns), bf16),
            pltpu.VMEM((4, 16, rows_owned, width), bf16),
            pltpu.VMEM((4, 15, rows_owned, width), bf16),
            pltpu.VMEM((8, 8, 768), bf16),
            pltpu.VMEM((8, 8, 768), bf16),
            dma((3,)), dma((3,)), dma((8, CHUNKS)), dma((8, CHUNKS)), dma((4, 16)), dma((4, 15)), dma((8,)), dma((8,)),
            *attention_scratch(keys.shape[0], keys.shape[1]),
        ],
        compiler_params=pltpu.CompilerParams(
            collective_id=0, has_side_effects=True, vmem_limit_bytes=60 * 1024 * 1024
        ),
        name="step",
    )(lens, queries, keys, values, weight, fresh, keyed)


def parcel_keys(accepted, dest):
    target = dest // 64
    landing = dest % 64
    beam_index = jnp.arange(64, dtype=jnp.int32)
    earlier = (target[None, :] == target[:, None]) & (beam_index[None, :] < beam_index[:, None])
    position = jnp.sum(earlier.astype(jnp.int32), 1)
    send_slot = target * 8 + position
    order = jnp.arange(8, dtype=jnp.int32)
    draft = jnp.arange(5, dtype=jnp.int32)
    shape = (8, 64, 5)
    slot = jnp.broadcast_to(send_slot[None, :, None], shape)
    on = (order[:, None, None] == draft[None, None, :]) & (draft[None, None, :] < accepted[None, :, None])
    first = (order[:, None, None] == 5) & (draft[None, None, :] == 0)
    keys = jnp.where(on | first, slot, -1)
    keys = jnp.where(order[:, None, None] == 6, landing[None, :, None], keys)
    return keys.reshape(8, 320)


def shards(queries, new_kv, cache_keys, cache_values, cache_lens, accepted, dest, out_weight):
    beams, _, span, size = cache_keys.shape
    mixed, moved = step(
        cache_lens, queries, cache_keys.reshape(beams, span, size), cache_values.reshape(beams, span, size),
        out_weight, new_kv, parcel_keys(accepted, dest),
    )
    return mixed, moved.transpose(1, 0, 2)


def solution(mesh):
    placed = (
        P("row", "mp"),
        P("row", "mp"),
        P("row", "mp", None, None),
        P("row", "mp", None, None),
        P("row"),
        P("row"),
        P("row"),
        P("mp", "row"),
    )
    return jax.shard_map(
        shards,
        mesh=mesh,
        in_specs=placed,
        out_specs=(P("mp", "row"), P("row", None, "mp")),
        check_vma=False,
    )
```

time: 175 us -> 143 us (0.82)
  Pallas kernels: 90.5 us -> 134 us
  waiting for transfers between devices: 30.7 us -> 0 us
  matrix products: 17 us -> 0 us
  other arithmetic: 17.1 us -> 1.63 us
  starting transfers between devices: 6.05 us -> 0 us
  local copies, waits for them, and re-layouts: 10.5 us -> 5.4 us
    pallas_call x1, Pallas kernels: 90.5 us -> 134 us  [step(): pl.pallas_call(step_kernel, out_shape=(jax.ShapeDtypeStruct((rows_owned,...]
    ppermute x5 -> x0, waiting for transfers between devices: 30.7 us -> none  [partner(): return lax.ppermute(block, axis, route)]
    dot_general x4 -> x0, matrix products: 17 us -> none  [the longest x1 6.47 us: attend(): jnp.einsum('btjd,bsid->bstji', query_block, cache_keys, preferred_element...]
    reduce_sum x4 -> x0, other arithmetic: 10.7 us -> none  [the longest x1 6.68 us: attend(): jnp.sum(cache_weights.astype(jnp.float32), -1)]
    ppermute x5 -> x0, starting transfers between devices: 6.05 us -> none  [partner(): return lax.ppermute(block, axis, route)]
    another operation x6 -> x0, local copies, waits for them, and re-layouts: 2.24 us -> none
    unnamed x12 -> x2, local copies, waits for them, and re-layouts: 5.54 us -> 3.51 us
    unnamed x1 -> x0, other arithmetic: 1.76 us -> none
  transfers between devices with their start and end apart: 5 -> 0, of which waited for: 2 -> 0; matrix products, arithmetic and copies ran while one was open for 8% -> 0% of each run, Pallas kernels for 0% -> 0%
where the time goes in v2:
time: 143 us; the launch traced here: 142 us
  Pallas kernels  134 us (94%)
  local copies, waits for them, and re-layouts  5.4 us (4%)
  other arithmetic  1.63 us (1%)
    pallas_call x1, Pallas kernels, step(): pl.pallas_call(step_kernel, out_shape=(jax.ShapeDtypeStruct((rows_owned,...  134 us
    unnamed x2, local copies, waits for them, and re-layouts  3.51 us

profile of v2, /device:TPU:14, one launch (start us, length us, event | category | flops | bytes accessed | tf_op | source)
XLA Modules:
  0.0 142.2 jit_solution(2471867322506190057)
XLA Ops:
  0.7 0.1 broadcast_and_fusion
  0.7 0.7 and_select_fusion.1
  1.4 0.2 convert_reduce_fusion
  1.6 0.1 broadcast_in_dim.50
  1.7 0.1 broadcast_in_dim.51
  1.8 0.1 broadcast_in_dim.47
  1.9 0.1 broadcast_in_dim.48
  2.0 0.7 lt.44
  2.8 0.1 lt.45
  2.9 0.1 lt.43
  3.1 0.2 and.49
  3.3 0.2 or.12
  3.5 0.7 select_select_fusion.keyed
  4.2 134.4 %step.1 = (bf16[160,2048]{1,0:T(8,128)(2,1)}, bf16[5,64,128]{2,1,0:T(8,128)(2,1)}) custom-call(s32[64]{0:T(128)} %lens.1, bf16[320,1024]{1,0:T(8,128)(2,1)} %queries.1, bf16[64,512,128]{2,1,0:T(8,128)(2,1)} %bitcast.5, bf16[64,512,128]{2,1,0:T(8,128)(2,1)} %bitcast.6, bf16[1024,2048]{1,0:T(8,128)(2,1)} %weight.1, bf16[320,128]{1,0:T(8,128)(2,1)} %fresh.1, ...), custom_call_target="tpu_custom_call" | custom-call | tf_op jit(solution)/shard_map/step/pallas_call | solution.py:513
  138.6 2.0 %copy.12 = bf16[160,2048]{1,0:T(8,128)(2,1)} copy(bf16[160,2048]{1,0:T(8,128)(2,1)} %get-tuple-element.10) | data formatting | bytes 1310720
  140.6 1.5 %copy.13 = bf16[64,5,128]{2,0,1:T(8,128)(2,1)} copy(bf16[64,5,128]{2,0,1:T(8,128)(2,1)} %bitcast.7) | data formatting | bytes 163840
  (9 shorter events, 0.1 us)

commit v3 on v2

v3 whole, which is shorter than its diff:
```python
import jax
import jax.numpy as jnp
from jax import lax
from jax.experimental import pallas as pl
from jax.experimental.pallas import tpu as pltpu
from jax.sharding import PartitionSpec as P

MESH = pl.DeviceIdType.MESH
masked_score = -1e30
LOG2E = 1.4426950408889634

TREES = ((0, 2, 1, 3), (2, 1, 3, 0), (1, 3, 0, 2), (3, 0, 2, 1))
WIDTHS = (512, 512, 512, 512)
STARTS = tuple(sum(WIDTHS[:tree]) for tree in range(4))
STEP_BASE = (0, 8, 12, 14)
LAG = 4
FIRST_UNIT = 3
CHUNKS = 4
UNROLL = 4
AHEAD = 2
GATHER_KINDS = (
    "to_right", "to_left", "to_sibling", "share_right", "share_left", "share_far", "pass_left", "pass_right",
)


def bits_of(place):
    y, z = place // 4, place % 4
    return (((y + 1) // 2) % 2, y // 2, ((z + 1) // 2) % 2, z // 2)


def along(place, direction):
    y, z = place // 4, place % 4
    if direction == 0:
        y = y + 1 - 2 * (y % 2)
    elif direction == 1:
        y = 3 - y
    elif direction == 2:
        z = z + 1 - 2 * (z % 2)
    else:
        z = 3 - z
    return y * 4 + z


def all_of(terms):
    result = terms[0]
    for term in terms[1:]:
        result = jnp.logical_and(result, term)
    return result


def within(number, low, high):
    return jnp.logical_and(number >= low, number < high)


def remote(source, target, send_sem, recv_sem, device):
    return pltpu.make_async_remote_copy(
        src_ref=source, dst_ref=target, send_sem=send_sem, recv_sem=recv_sem,
        device_id=device, device_id_type=MESH,
    )


def dot_nt(left, right):
    return lax.dot_general(
        left, right, (((1,), (1,)), ((), ())), preferred_element_type=jnp.float32
    )


def chunk_of(turn):
    return (turn % 2) * 2 + turn // 2


class Attention:
    def __init__(self, lens, queries, fresh, keys, values, side, pair, refs):
        self.lens, self.queries, self.fresh, self.keys, self.values = lens, queries, fresh, keys, values
        self.side, self.pair = side, pair
        (
            self.query_rows, self.query_out, self.query_in, self.fresh_in, self.key_slots, self.value_slots,
            self.sum_own, self.top_own, self.mass_own, self.sum_fresh, self.top_fresh, self.mass_fresh,
            self.part_out, self.part_in, self.stat_out, self.stat_in,
            self.cache_sem, self.fresh_sem, self.query_send, self.query_recv,
            self.part_send, self.part_recv, self.stat_send, self.stat_recv,
        ) = refs
        self.per = keys.shape[0] // CHUNKS
        self.tokens = self.per * 5
        self.span = keys.shape[1]
        self.scale = 128 ** -0.5 * LOG2E

    def cache_copies(self, turn):
        beams = pl.ds(chunk_of(turn) * self.per, self.per)
        slot = turn % 2
        return (
            pltpu.make_async_copy(self.keys.at[beams], self.key_slots.at[slot], self.cache_sem.at[0, slot]),
            pltpu.make_async_copy(self.values.at[beams], self.value_slots.at[slot], self.cache_sem.at[1, slot]),
        )

    def query_message(self, turn):
        return remote(
            self.query_out.at[turn], self.query_in.at[turn], self.query_send.at[turn], self.query_recv.at[turn], self.pair
        )

    def part_message(self, turn):
        return remote(
            self.part_out.at[turn], self.part_in.at[turn], self.part_send.at[turn], self.part_recv.at[turn], self.pair
        )

    def stat_message(self, turn):
        return remote(
            self.stat_out.at[turn], self.stat_in.at[turn], self.stat_send.at[turn], self.stat_recv.at[turn], self.pair
        )

    def fresh_message(self):
        return remote(self.fresh, self.fresh_in, self.fresh_sem.at[0], self.fresh_sem.at[1], self.pair)

    def send_query(self, turn):
        tokens = self.tokens
        at = pl.ds(pl.multiple_of(chunk_of(turn) * tokens, 16), tokens)
        for head in range(8):
            self.query_rows[turn, pl.ds(head, tokens, stride=8), :] = self.queries[
                at, head * 128 : (head + 1) * 128
            ].astype(jnp.float32)
        for part in range(self.per):
            self.query_out[turn, part] = self.query_rows[turn, part * 40 : part * 40 + 40, :].astype(jnp.bfloat16)
        self.query_message(turn).start()

    def attend(self, turn):
        chunk, slot, per = chunk_of(turn), turn % 2, self.per
        tokens, scale = self.tokens, self.scale
        rows = per * 40
        row_of = lax.broadcasted_iota(jnp.int32, (rows, tokens), 0)
        key_of = lax.broadcasted_iota(jnp.int32, (rows, tokens), 1)
        fresh_valid = jnp.logical_and(
            row_of // 40 == key_of // 5, (row_of % 40) // 8 >= key_of % 5
        )
        lane = lax.broadcasted_iota(jnp.int32, (40, 128), 1)
        spot = lax.broadcasted_iota(jnp.int32, (80, self.span), 1) + self.side * self.span

        at = pl.ds(pl.multiple_of(chunk * tokens, 16), tokens)
        mine, theirs = self.fresh[at, :], self.fresh_in[at, :]
        even = self.side == 0
        fresh_keys = jnp.where(even, mine, theirs)
        fresh_values = jnp.where(even, theirs, mine)
        scores = dot_nt(self.query_rows[turn].astype(jnp.bfloat16), fresh_keys)
        scores = jnp.where(fresh_valid, scores, masked_score)
        highest = jnp.max(scores, 1, keepdims=True)
        weights = jnp.exp2((scores - highest) * scale).astype(jnp.bfloat16)
        sums = jnp.dot(
            weights, jnp.concatenate([fresh_values, jnp.ones_like(fresh_values)], 1),
            preferred_element_type=jnp.float32,
        )
        self.sum_fresh[...] = sums[:, :128]
        self.mass_fresh[...] = sums[:, 128:]
        self.top_fresh[...] = jnp.broadcast_to(highest * scale, (rows, 128))

        for copy in self.cache_copies(turn):
            copy.wait()

        @pl.when(turn + 1 < CHUNKS)
        def _():
            for copy in self.cache_copies(turn + 1):
                copy.start()

        self.query_message(turn).wait_recv()

        def beams_step(group, stat):
            for member in range(UNROLL):
                local = group * UNROLL + member
                at = pl.multiple_of(local * 40, 8)
                block = jnp.concatenate(
                    [
                        self.query_rows[turn, pl.ds(at, 40), :],
                        self.query_in[turn, local].astype(jnp.float32),
                    ],
                    0,
                ).astype(jnp.bfloat16)
                scores = dot_nt(block, self.key_slots[slot, local])
                scores = jnp.where(spot < self.lens[chunk * per + local], scores, masked_score)
                highest = jnp.max(scores, 1, keepdims=True)
                weights = jnp.exp2((scores - highest) * scale).astype(jnp.bfloat16)
                value = self.value_slots[slot, local]
                sums = jnp.dot(
                    weights, jnp.concatenate([value, jnp.ones_like(value)], 1),
                    preferred_element_type=jnp.float32,
                )
                top = jnp.broadcast_to(highest * scale, (80, 128))
                self.part_out[turn, local] = (sums[40:, :128] / sums[40:, 128:]).astype(jnp.bfloat16)
                stat = jnp.where(lane == local, top[40:] + jnp.log2(sums[40:, 128:]), stat)
                near = self.top_fresh[pl.ds(at, 40), :]
                summit = jnp.maximum(top[:40], near)
                here = jnp.exp2(top[:40] - summit)
                there = jnp.exp2(near - summit)
                self.sum_own[turn, pl.ds(at, 40), :] = (
                    sums[:40, :128] * here + self.sum_fresh[pl.ds(at, 40), :] * there
                )
                self.mass_own[turn, pl.ds(at, 40), :] = (
                    sums[:40, 128:] * here + self.mass_fresh[pl.ds(at, 40), :] * there
                )
                self.top_own[turn, pl.ds(at, 40), :] = summit
            return stat

        self.stat_out[turn] = lax.fori_loop(0, per // UNROLL, beams_step, jnp.zeros((40, 128), jnp.float32))
        self.part_message(turn).start()
        self.stat_message(turn).start()

    def combine(self, turn):
        self.part_message(turn).wait_recv()
        self.stat_message(turn).wait_recv()
        lane = lax.broadcasted_iota(jnp.int32, (40, 128), 1)

        def beams_step(group, inner):
            stat = self.stat_in[turn]
            for member in range(UNROLL):
                local = group * UNROLL + member
                at = pl.multiple_of(local * 40, 8)
                other = jnp.sum(jnp.where(lane == local, stat, 0.0), 1, keepdims=True)
                top = self.top_own[turn, pl.ds(at, 40), :]
                summit = jnp.maximum(top, other)
                here = jnp.exp2(top - summit)
                there = jnp.exp2(other - summit)
                total = (
                    self.sum_own[turn, pl.ds(at, 40), :] * here + self.part_in[turn, local].astype(jnp.float32) * there
                )
                mass = self.mass_own[turn, pl.ds(at, 40), :] * here + there
                self.sum_fresh[pl.ds(at, 40), :] = total / mass
            return inner

        lax.fori_loop(0, self.per // UNROLL, beams_step, 0)
        return self.sum_fresh

    def settle(self):
        self.fresh_message().wait_send()

        def one(turn, carry):
            self.query_message(turn).wait_send()
            self.part_message(turn).wait_send()
            self.stat_message(turn).wait_send()
            return carry

        lax.fori_loop(0, CHUNKS, one, 0)


def attention_scratch(beams, span):
    per = beams // CHUNKS
    bf16, f32 = jnp.bfloat16, jnp.float32
    dma = pltpu.SemaphoreType.DMA
    return [
        pltpu.VMEM((CHUNKS, per * 40, 128), f32),
        pltpu.VMEM((CHUNKS, per, 40, 128), bf16),
        pltpu.VMEM((CHUNKS, per, 40, 128), bf16),
        pltpu.VMEM((beams * 5, 128), bf16),
        pltpu.VMEM((2, per, span, 128), bf16),
        pltpu.VMEM((2, per, span, 128), bf16),
        pltpu.VMEM((CHUNKS, per * 40, 128), f32),
        pltpu.VMEM((CHUNKS, per * 40, 128), f32),
        pltpu.VMEM((CHUNKS, per * 40, 128), f32),
        pltpu.VMEM((per * 40, 128), f32),
        pltpu.VMEM((per * 40, 128), f32),
        pltpu.VMEM((per * 40, 128), f32),
        pltpu.VMEM((CHUNKS, per, 40, 128), bf16),
        pltpu.VMEM((CHUNKS, per, 40, 128), bf16),
        pltpu.VMEM((CHUNKS, 40, 128), f32),
        pltpu.VMEM((CHUNKS, 40, 128), f32),
        dma((2, 2)), dma((2,)), dma((CHUNKS,)), dma((CHUNKS,)), dma((CHUNKS,)), dma((CHUNKS,)), dma((CHUNKS,)), dma((CHUNKS,)),
    ]


def row_keys(accepted, dest):
    beams = dest.shape[1]
    target = (dest // beams).astype(jnp.float32)
    landing = (dest % beams).astype(jnp.float32)
    over = lax.broadcasted_iota(jnp.int32, (beams, beams), 0)
    lane = lax.broadcasted_iota(jnp.int32, (beams, beams), 1)
    wide = jnp.broadcast_to(target, (beams, beams))
    tall = jnp.sum(jnp.where(over == lane, wide, 0.0), 1, keepdims=True)
    earlier = jnp.logical_and(tall == wide, over < lane)
    position = jnp.sum(jnp.where(earlier, 1.0, 0.0), 0, keepdims=True)
    place = target * (beams // 8) + position
    numbers = jnp.concatenate(
        [place, accepted.astype(jnp.float32), landing, jnp.zeros((5, beams), jnp.float32)], 0
    )
    spread = lax.broadcasted_iota(jnp.int32, (beams, beams * 5), 1) // 5 == lax.broadcasted_iota(
        jnp.int32, (beams, beams * 5), 0
    )
    rows = jnp.dot(
        numbers.astype(jnp.bfloat16), spread.astype(jnp.bfloat16), preferred_element_type=jnp.float32
    )
    return rows[0:1], rows[1:2], rows[2:3]


def step_kernel(
    lens, queries, keys, values, weight, fresh, accepted, dest, mixed, next_kv,
    gathered, weight_here, held_0, held_1, held_2, held_3, inbox_0, inbox_1, inbox_2, inbox_3, parcels, arrived,
    local_sem, far_send, gather_recv, tree_send, tree_recv, parcel_send, parcel_recv, *attention_refs,
):
    row, mp = lax.axis_index("row"), lax.axis_index("mp")
    x, core = row // 2, row % 2
    sibling = {"row": x * 2 + 1 - core, "mp": mp}
    right = {"row": ((x + 1) % 4) * 2 + core, "mp": mp}
    left = {"row": ((x + 3) % 4) * 2 + core, "mp": mp}
    pair = {"row": row, "mp": along(mp, 2)}
    held = (held_0, held_1, held_2, held_3)
    inbox = (inbox_0, inbox_1, inbox_2, inbox_3)
    work = Attention(lens, queries, fresh, keys, values, mp % 2, pair, attention_refs)
    for copy in work.cache_copies(0):
        copy.start()
    weight_copy = pltpu.make_async_copy(weight, weight_here, local_sem.at[0])
    weight_copy.start()

    barrier = pltpu.get_barrier_semaphore()
    for step in range(1, 8):
        pl.semaphore_signal(
            barrier, inc=1, device_id={"row": (row + step) % 8, "mp": mp}, device_id_type=MESH
        )
    for direction in range(4):
        pl.semaphore_signal(
            barrier, inc=1, device_id={"row": row, "mp": along(mp, direction)}, device_id_type=MESH
        )
    pl.semaphore_wait(barrier, 11)

    def send_first(turn, carry):
        work.send_query(turn)

        @pl.when(turn == 0)
        def _():
            work.fresh_message().start()

        return carry

    lax.fori_loop(0, AHEAD, send_first, 0)

    tokens = gathered.shape[2]
    half = gathered.shape[3] // 2

    def gather_message(kind, turn):
        source, target, device = {
            "to_right": (0, 3, right), "to_left": (0, 2, left), "to_sibling": (0, 1, sibling),
            "share_right": (2, 4, sibling), "share_left": (3, 5, sibling), "share_far": (6, 7, sibling),
            "pass_left": (2, 6, left), "pass_right": (3, 6, right),
        }[kind]
        number = GATHER_KINDS.index(kind)
        send, recv = far_send.at[number, turn], gather_recv.at[number, turn]
        if kind in ("pass_left", "pass_right"):
            part = pl.ds(0 if kind == "pass_left" else half, half)
            return remote(
                gathered.at[source, turn, :, part], gathered.at[target, turn, :, part], send, recv, device
            )
        return remote(gathered.at[source, turn], gathered.at[target, turn], send, recv, device)

    def publish(turn, rows):
        for head in range(8):
            gathered[0, turn, :, head * 128 : (head + 1) * 128] = rows[pl.ds(head, tokens, stride=8), :].astype(
                jnp.bfloat16
            )
        for kind in ("to_right", "to_left", "to_sibling"):
            gather_message(kind, turn).start()

    def near(turn):
        gather_message("to_left", turn).wait_recv()
        gather_message("pass_left", turn).start()
        gather_message("share_right", turn).start()
        gather_message("to_right", turn).wait_recv()
        gather_message("pass_right", turn).start()
        gather_message("share_left", turn).start()

    def far(turn):
        gather_message("pass_left", turn).wait_recv()
        gather_message("pass_right", turn).wait_recv()
        gather_message("share_far", turn).start()

    place_row, kept_row, landing_row = row_keys(accepted[...], dest[...])
    place = lax.broadcasted_iota(jnp.int32, (64, 320), 0).astype(jnp.float32)
    draft_of = (lax.broadcasted_iota(jnp.int32, (1, 320), 1) % 5).astype(jnp.float32)
    fresh_rows = fresh[...]
    columns = []
    for draft in range(5):
        taken = jnp.where(jnp.logical_and(draft_of == draft, kept_row > draft), place_row, -1.0)
        columns.append(
            jnp.dot(
                (taken == place).astype(jnp.bfloat16), fresh_rows, preferred_element_type=jnp.float32
            ).astype(jnp.bfloat16)
        )
    first = jnp.where(draft_of == 0, place_row, -1.0)
    label = jnp.sum(jnp.where(first == place, landing_row, 0.0), 1, keepdims=True)
    columns.append(jnp.broadcast_to(label, (64, 128)).astype(jnp.bfloat16))
    for block in range(8):
        for part, column in enumerate(columns):
            parcels[block, :, pl.ds(part * 128, 128)] = column[block * 8 : block * 8 + 8]
    own_parcel = pltpu.make_async_copy(parcels.at[row], arrived.at[row], local_sem.at[1])
    own_parcel.start()
    for step in range(1, 8):
        target = (row + step) % 8
        remote(
            parcels.at[target], arrived.at[row], parcel_send.at[step], parcel_recv.at[row],
            {"row": target, "mp": mp},
        ).start()
    work.fresh_message().wait_recv()
    weight_copy.wait()

    my_bits = bits_of(mp)

    def tree_message(tree, step, phase, block):
        order = TREES[tree]
        rest = bits_of(block)
        index = STEP_BASE[step]
        for power, direction in enumerate(order[step + 1 :]):
            index = index + rest[direction] * (1 << power)
        index = phase * 15 + index
        return remote(
            held[tree].at[phase * 16 + block], inbox[tree].at[index], tree_send.at[tree, phase * 16 + block],
            tree_recv.at[tree, index], {"row": row, "mp": along(mp, order[step])},
        ), index

    def first_block(slot):
        shift = jnp.where(slot < 2, 0, jnp.where(slot >= 6, 2, jnp.where(slot % 2 == 0, 1, 3)))
        other = jnp.where(slot < 6, jnp.where(slot < 2, slot, jnp.where(slot >= 4, 1, 0)), slot - 6)
        owner = ((x + shift) % 4) * 2 + jnp.where(other == 1, 1 - core, core)
        return owner * 2

    def block_of(couple, piece):
        return first_block(couple * 2 + piece // 2) + piece % 2

    def product_unit(unit):
        phase, couple = unit // 4, unit % 4
        early = phase * 2

        @pl.when(couple == 0)
        def _():
            for turn in (early, early + 1):
                gather_message("to_sibling", turn).wait_recv()

        @pl.when(couple == 2)
        def _():
            for turn in (early, early + 1):
                gather_message("share_right", turn).wait_recv()
                gather_message("share_left", turn).wait_recv()

        @pl.when(couple == 3)
        def _():
            for turn in (early, early + 1):
                gather_message("share_far", turn).wait_recv()

        operand = gathered[pl.ds(couple * 2, 2), pl.ds(early, 2)].reshape(4 * tokens, gathered.shape[3])
        for tree in range(4):
            product = jnp.dot(
                operand, weight_here[:, STARTS[tree] : STARTS[tree] + WIDTHS[tree]],
                preferred_element_type=jnp.float32,
            ).astype(jnp.bfloat16)
            direction = TREES[tree][0]
            for piece in range(4):
                block = block_of(couple, piece)
                held[tree][phase * 16 + block] = product[piece * tokens : (piece + 1) * tokens]

                @pl.when(bits_of(block)[direction] != my_bits[direction])
                def _(tree=tree, block=block):
                    tree_message(tree, 0, phase, block)[0].start()

    def receive_unit(step, unit):
        phase, couple = unit // 4, unit % 4

        def one(piece, carry):
            block = block_of(couple, piece)
            theirs = bits_of(block)
            for tree in range(4):
                order = TREES[tree]
                same = all_of([theirs[d] == my_bits[d] for d in order[: step + 1]])

                @pl.when(same)
                def _(tree=tree, order=order):
                    message, index = tree_message(tree, step, phase, block)
                    message.wait_recv()
                    at = phase * 16 + block
                    total = held[tree][at].astype(jnp.float32) + inbox[tree][index].astype(jnp.float32)
                    if step == 3:
                        out = pl.ds(pl.multiple_of(phase * tokens, 16), tokens)
                        mixed[out, STARTS[tree] : STARTS[tree] + WIDTHS[tree]] = total.astype(jnp.bfloat16)
                    else:
                        held[tree][at] = total.astype(jnp.bfloat16)
                        onward = order[step + 1]

                        @pl.when(theirs[onward] != my_bits[onward])
                        def _():
                            tree_message(tree, step + 1, phase, block)[0].start()

            return carry

        lax.fori_loop(0, 4, one, 0)

    def tick(time, carry):
        for step in (3, 2, 1, 0):
            unit = time - FIRST_UNIT - LAG * (step + 1)

            @pl.when(within(unit, 0, 8))
            def _(step=step, unit=unit):
                receive_unit(step, unit)

        @pl.when(within(time - FIRST_UNIT, 0, 8))
        def _():
            product_unit(time - FIRST_UNIT)

        @pl.when(within(time, 0, CHUNKS))
        def _():
            work.attend(time)

            @pl.when(time + AHEAD < CHUNKS)
            def _():
                work.send_query(time + AHEAD)

        @pl.when(within(time - 3, 0, CHUNKS))
        def _():
            far(time - 3)

        @pl.when(within(time - 2, 0, CHUNKS))
        def _():
            near(time - 2)

        @pl.when(within(time - 1, 0, CHUNKS))
        def _():
            publish(time - 1, work.combine(time - 1))

        return carry

    lax.fori_loop(0, FIRST_UNIT + 8 + 4 * LAG, tick, 0)

    own_parcel.wait()
    for step in range(1, 8):
        source = (row + 8 - step) % 8
        remote(
            parcels.at[source], arrived.at[source], parcel_send.at[step], parcel_recv.at[source],
            {"row": source, "mp": mp},
        ).wait_recv()
    rows = jnp.concatenate([arrived[block] for block in range(8)], 0)
    slots = lax.broadcasted_iota(jnp.int32, (64, 64), 1).astype(jnp.float32)
    placer = (rows[:, 640:704].astype(jnp.float32) == slots).astype(jnp.bfloat16)
    placed = lax.dot_general(
        placer, rows[:, :640], (((0,), (0,)), ((), ())), preferred_element_type=jnp.float32
    ).astype(jnp.bfloat16)
    for draft in range(5):
        next_kv[draft] = placed[:, draft * 128 : (draft + 1) * 128]

    def settle_gather(turn, carry):
        for kind in GATHER_KINDS:
            gather_message(kind, turn).wait_send()
        return carry

    lax.fori_loop(0, CHUNKS, settle_gather, 0)
    work.settle()
    for step in range(1, 8):
        target = (row + step) % 8
        remote(
            parcels.at[target], arrived.at[row], parcel_send.at[step], parcel_recv.at[row],
            {"row": target, "mp": mp},
        ).wait_send()

    def settle(block, carry):
        @pl.when(block % 16 != mp)
        def _():
            for tree in range(4):
                remote(
                    held[tree].at[block], inbox[tree].at[0], tree_send.at[tree, block], tree_recv.at[tree, 0],
                    {"row": row, "mp": along(mp, 0)},
                ).wait_send()

        return carry

    lax.fori_loop(0, 32, settle, 0)


def step(lens, queries, keys, values, weight, fresh, accepted, dest):
    tokens, depth = queries.shape
    columns = weight.shape[1]
    beams, span = keys.shape[0], keys.shape[1]
    rows_owned = tokens // 2
    piece = tokens // CHUNKS
    bf16 = jnp.bfloat16
    dma = pltpu.SemaphoreType.DMA
    vmem = pl.BlockSpec(memory_space=pltpu.VMEM)
    hbm = pl.BlockSpec(memory_space=pl.ANY)
    return pl.pallas_call(
        step_kernel,
        out_shape=(
            jax.ShapeDtypeStruct((rows_owned, columns), bf16),
            jax.ShapeDtypeStruct((5, beams, 128), bf16),
        ),
        in_specs=[pl.BlockSpec(memory_space=pltpu.SMEM), vmem, hbm, hbm, hbm, vmem, vmem, vmem],
        out_specs=(vmem, vmem),
        scratch_shapes=[
            pltpu.VMEM((8, CHUNKS, piece, depth), bf16),
            pltpu.VMEM((depth, columns), bf16),
            *[pltpu.VMEM((32, piece, width), bf16) for width in WIDTHS],
            *[pltpu.VMEM((30, piece, width), bf16) for width in WIDTHS],
            pltpu.VMEM((8, 8, 768), bf16),
            pltpu.VMEM((8, 8, 768), bf16),
            dma((2,)), dma((8, CHUNKS)), dma((8, CHUNKS)), dma((4, 32)), dma((4, 30)), dma((8,)), dma((8,)),
            *attention_scratch(beams, span),
        ],
        compiler_params=pltpu.CompilerParams(
            collective_id=0, has_side_effects=True, vmem_limit_bytes=60 * 1024 * 1024
        ),
        name="step",
    )(lens, queries, keys, values, weight, fresh, accepted, dest)


def shards(queries, new_kv, cache_keys, cache_values, cache_lens, accepted, dest, out_weight):
    beams, _, span, size = cache_keys.shape
    mixed, moved = step(
        cache_lens, queries, cache_keys.reshape(beams, span, size), cache_values.reshape(beams, span, size),
        out_weight, new_kv, accepted.reshape(1, beams), dest.reshape(1, beams),
    )
    return mixed, moved.transpose(1, 0, 2)


def solution(mesh):
    placed = (
        P("row", "mp"),
        P("row", "mp"),
        P("row", "mp", None, None),
        P("row", "mp", None, None),
        P("row"),
        P("row"),
        P("row"),
        P("mp", "row"),
    )
    return jax.shard_map(
        shards,
        mesh=mesh,
        in_specs=placed,
        out_specs=(P("mp", "row"), P("row", None, "mp")),
        check_vma=False,
    )
```

time: 143 us -> 115 us (0.80)
  Pallas kernels: 134 us -> 111 us
  local copies, waits for them, and re-layouts: 5.4 us -> 3.51 us
  other arithmetic: 1.63 us -> 0 us
    pallas_call x1, Pallas kernels: 134 us -> 111 us  [step(): pl.pallas_call(step_kernel, out_shape=(jax.ShapeDtypeStruct((rows_owned,...]
where the time goes in v3:
time: 115 us
  Pallas kernels  111 us (97%)
  local copies, waits for them, and re-layouts  3.51 us (3%)
    pallas_call x1, Pallas kernels, step(): pl.pallas_call(step_kernel, out_shape=(jax.ShapeDtypeStruct((rows_owned,...  111 us
    unnamed x2, local copies, waits for them, and re-layouts  3.51 us

profile of v3, /device:TPU:14, one launch (start us, length us, event | category | flops | bytes accessed | tf_op | source)
XLA Modules:
  0.0 114.8 jit_solution(14355268590734538764)
XLA Ops:
  0.6 110.7 %step.1 = (bf16[160,2048]{1,0:T(8,128)(2,1)}, bf16[5,64,128]{2,1,0:T(8,128)(2,1)}) custom-call(s32[64]{0:T(128)} %lens.1, bf16[320,1024]{1,0:T(8,128)(2,1)} %queries.1, bf16[64,512,128]{2,1,0:T(8,128)(2,1)} %bitcast.5, bf16[64,512,128]{2,1,0:T(8,128)(2,1)} %bitcast.6, bf16[1024,2048]{1,0:T(8,128)(2,1)} %weight.1, bf16[320,128]{1,0:T(8,128)(2,1)} %fresh.1, ...), custom_call_target="tpu_custom_call" | custom-call | tf_op jit(solution)/shard_map/step/pallas_call | solution.py:577
  111.3 2.0 %copy.12 = bf16[160,2048]{1,0:T(8,128)(2,1)} copy(bf16[160,2048]{1,0:T(8,128)(2,1)} %get-tuple-element.8) | data formatting | bytes 1310720
  113.3 1.5 %copy.13 = bf16[64,5,128]{2,0,1:T(8,128)(2,1)} copy(bf16[64,5,128]{2,0,1:T(8,128)(2,1)} %bitcast.7) | data formatting | bytes 163840

commit v4 on v3

--- a/solution.py
+++ b/solution.py
@@ -13,11 +13,12 @@
 WIDTHS = (512, 512, 512, 512)
 STARTS = tuple(sum(WIDTHS[:tree]) for tree in range(4))
 STEP_BASE = (0, 8, 12, 14)
-LAG = 4
+RECEIVES = ((7, 8, 9, 10), (8, 9, 10, 11))
 FIRST_UNIT = 3
 CHUNKS = 4
-UNROLL = 4
-AHEAD = 2
+UNROLL = 8
+AHEAD = 3
+BACK = 2
 GATHER_KINDS = (
     "to_right", "to_left", "to_sibling", "share_right", "share_left", "share_far", "pass_left", "pass_right",
 )
@@ -39,13 +40,6 @@
     else:
         z = 3 - z
     return y * 4 + z
-
-
-def all_of(terms):
-    result = terms[0]
-    for term in terms[1:]:
-        result = jnp.logical_and(result, term)
-    return result
 
 
 def within(number, low, high):
@@ -396,17 +390,16 @@
     weight_copy.wait()
 
     my_bits = bits_of(mp)
-
-    def tree_message(tree, step, phase, block):
-        order = TREES[tree]
-        rest = bits_of(block)
-        index = STEP_BASE[step]
-        for power, direction in enumerate(order[step + 1 :]):
-            index = index + rest[direction] * (1 << power)
-        index = phase * 15 + index
+    y, z = mp // 4, mp % 4
+    over_y = (y, along(mp, 0) // 4, along(mp, 1) // 4, (y + 2) % 4)
+    over_z = (z, along(mp, 2) % 4, along(mp, 3) % 4, (z + 2) % 4)
+    partners = [along(mp, direction) for direction in range(4)]
+
+    def tree_message(tree, step, phase, block, rest):
+        index = phase * 15 + STEP_BASE[step] + rest
         return remote(
-            held[tree].at[phase * 16 + block], inbox[tree].at[index], tree_send.at[tree, phase * 16 + block],
-            tree_recv.at[tree, index], {"row": row, "mp": along(mp, order[step])},
+            held[tree].at[phase * 16 + block], inbox[tree].at[index], tree_send.at[tree, index],
+            tree_recv.at[tree, index], {"row": row, "mp": partners[TREES[tree][step]]},
         ), index
 
     def first_block(slot):
@@ -439,63 +432,44 @@
                 gather_message("share_far", turn).wait_recv()
 
         operand = gathered[pl.ds(couple * 2, 2), pl.ds(early, 2)].reshape(4 * tokens, gathered.shape[3])
+        blocks = [block_of(couple, piece) for piece in range(4)]
+        across = [[(a + b) % 2 for a, b in zip(bits_of(block), my_bits)] for block in blocks]
         for tree in range(4):
             product = jnp.dot(
                 operand, weight_here[:, STARTS[tree] : STARTS[tree] + WIDTHS[tree]],
                 preferred_element_type=jnp.float32,
             ).astype(jnp.bfloat16)
-            direction = TREES[tree][0]
+            order = TREES[tree]
             for piece in range(4):
-                block = block_of(couple, piece)
+                block, apart = blocks[piece], across[piece]
                 held[tree][phase * 16 + block] = product[piece * tokens : (piece + 1) * tokens]
 
-                @pl.when(bits_of(block)[direction] != my_bits[direction])
-                def _(tree=tree, block=block):
-                    tree_message(tree, 0, phase, block)[0].start()
-
-    def receive_unit(step, unit):
-        phase, couple = unit // 4, unit % 4
-
-        def one(piece, carry):
-            block = block_of(couple, piece)
-            theirs = bits_of(block)
+                @pl.when(apart[order[0]] == 1)
+                def _(tree=tree, block=block, apart=apart, order=order):
+                    rest = apart[order[1]] + 2 * apart[order[2]] + 4 * apart[order[3]]
+                    tree_message(tree, 0, phase, block, rest)[0].start()
+
+    def receive_step(step, phase):
+        count = 1 << (3 - step)
+        for rest in sorted(range(count), key=lambda number: (1 - number % 2, number)):
             for tree in range(4):
-                order = TREES[tree]
-                same = all_of([theirs[d] == my_bits[d] for d in order[: step + 1]])
-
-                @pl.when(same)
-                def _(tree=tree, order=order):
-                    message, index = tree_message(tree, step, phase, block)
-                    message.wait_recv()
-                    at = phase * 16 + block
-                    total = held[tree][at].astype(jnp.float32) + inbox[tree][index].astype(jnp.float32)
-                    if step == 3:
-                        out = pl.ds(pl.multiple_of(phase * tokens, 16), tokens)
-                        mixed[out, STARTS[tree] : STARTS[tree] + WIDTHS[tree]] = total.astype(jnp.bfloat16)
-                    else:
-                        held[tree][at] = total.astype(jnp.bfloat16)
-                        onward = order[step + 1]
-
-                        @pl.when(theirs[onward] != my_bits[onward])
-                        def _():
-                            tree_message(tree, step + 1, phase, block)[0].start()
-
-            return carry
-
-        lax.fori_loop(0, 4, one, 0)
+                apart = [0, 0, 0, 0]
+                for later in range(step + 1, 4):
+                    apart[TREES[tree][later]] = (rest >> (later - step - 1)) & 1
+                block = over_y[apart[0] + 2 * apart[1]] * 4 + over_z[apart[2] + 2 * apart[3]]
+                message, index = tree_message(tree, step, phase, block, rest)
+                message.wait_recv()
+                at = phase * 16 + block
+                total = held[tree][at].astype(jnp.float32) + inbox[tree][index].astype(jnp.float32)
+                if step == 3:
+                    out = pl.ds(pl.multiple_of(phase * tokens, 16), tokens)
+                    mixed[out, STARTS[tree] : STARTS[tree] + WIDTHS[tree]] = total.astype(jnp.bfloat16)
+                else:
+                    held[tree][at] = total.astype(jnp.bfloat16)
+                    if rest % 2 == 1:
+                        tree_message(tree, step + 1, phase, block, rest // 2)[0].start()
 
     def tick(time, carry):
-        for step in (3, 2, 1, 0):
-            unit = time - FIRST_UNIT - LAG * (step + 1)
-
-            @pl.when(within(unit, 0, 8))
-            def _(step=step, unit=unit):
-                receive_unit(step, unit)
-
-        @pl.when(within(time - FIRST_UNIT, 0, 8))
-        def _():
-            product_unit(time - FIRST_UNIT)
-
         @pl.when(within(time, 0, CHUNKS))
         def _():
             work.attend(time)
@@ -504,21 +478,32 @@
             def _():
                 work.send_query(time + AHEAD)
 
-        @pl.when(within(time - 3, 0, CHUNKS))
-        def _():
-            far(time - 3)
-
-        @pl.when(within(time - 2, 0, CHUNKS))
-        def _():
-            near(time - 2)
-
-        @pl.when(within(time - 1, 0, CHUNKS))
-        def _():
-            publish(time - 1, work.combine(time - 1))
+        @pl.when(within(time - BACK - 2, 0, CHUNKS))
+        def _():
+            far(time - BACK - 2)
+
+        @pl.when(within(time - BACK - 1, 0, CHUNKS))
+        def _():
+            near(time - BACK - 1)
+
+        @pl.when(within(time - BACK, 0, CHUNKS))
+        def _():
+            publish(time - BACK, work.combine(time - BACK))
+
+        @pl.when(within(time - FIRST_UNIT, 0, 8))
+        def _():
+            product_unit(time - FIRST_UNIT)
+
+        for step in range(4):
+            early, late = (FIRST_UNIT + RECEIVES[phase][step] for phase in range(2))
+
+            @pl.when(jnp.logical_or(time == early, time == late))
+            def _(step=step, late=late):
+                receive_step(step, jnp.where(time == late, 1, 0))
 
         return carry
 
-    lax.fori_loop(0, FIRST_UNIT + 8 + 4 * LAG, tick, 0)
+    lax.fori_loop(0, FIRST_UNIT + 15, tick, 0)
 
     own_parcel.wait()
     for step in range(1, 8):
@@ -550,18 +535,15 @@
             {"row": target, "mp": mp},
         ).wait_send()
 
-    def settle(block, carry):
-        @pl.when(block % 16 != mp)
-        def _():
-            for tree in range(4):
-                remote(
-                    held[tree].at[block], inbox[tree].at[0], tree_send.at[tree, block], tree_recv.at[tree, 0],
-                    {"row": row, "mp": along(mp, 0)},
-                ).wait_send()
-
+    def settle(index, carry):
+        for tree in range(4):
+            remote(
+                held[tree].at[0], inbox[tree].at[index], tree_send.at[tree, index], tree_recv.at[tree, index],
+                {"row": row, "mp": partners[0]},
+            ).wait_send()
         return carry
 
-    lax.fori_loop(0, 32, settle, 0)
+    lax.fori_loop(0, 30, settle, 0)
 
 
 def step(lens, queries, keys, values, weight, fresh, accepted, dest):
@@ -589,7 +571,7 @@
             *[pltpu.VMEM((30, piece, width), bf16) for width in WIDTHS],
             pltpu.VMEM((8, 8, 768), bf16),
             pltpu.VMEM((8, 8, 768), bf16),
-            dma((2,)), dma((8, CHUNKS)), dma((8, CHUNKS)), dma((4, 32)), dma((4, 30)), dma((8,)), dma((8,)),
+            dma((2,)), dma((8, CHUNKS)), dma((8, CHUNKS)), dma((4, 30)), dma((4, 30)), dma((8,)), dma((8,)),
             *attention_scratch(beams, span),
         ],
         compiler_params=pltpu.CompilerParams(
@@ -599,12 +581,32 @@
     )(lens, queries, keys, values, weight, fresh, accepted, dest)
 
 
+def hand_on_kernel(mixed, moved, mixed_out, moved_out):
+    mixed_out[...] = mixed[...]
+    moved_out[...] = moved[...]
+
+
+def hand_on(mixed, moved):
+    vmem = pl.BlockSpec(memory_space=pltpu.VMEM)
+    return pl.pallas_call(
+        hand_on_kernel,
+        out_shape=(
+            jax.ShapeDtypeStruct(mixed.shape, mixed.dtype),
+            jax.ShapeDtypeStruct(moved.shape, moved.dtype),
+        ),
+        in_specs=[vmem, vmem],
+        out_specs=(vmem, vmem),
+        name="hand_on",
+    )(mixed, moved)
+
+
 def shards(queries, new_kv, cache_keys, cache_values, cache_lens, accepted, dest, out_weight):
     beams, _, span, size = cache_keys.shape
     mixed, moved = step(
         cache_lens, queries, cache_keys.reshape(beams, span, size), cache_values.reshape(beams, span, size),
         out_weight, new_kv, accepted.reshape(1, beams), dest.reshape(1, beams),
     )
+    mixed, moved = hand_on(mixed, moved)
     return mixed, moved.transpose(1, 0, 2)
 
 

time: 115 us -> 109 us (0.948); the launches traced: 115 us -> 108 us
  Pallas kernels: 111 us -> 107 us
  local copies, waits for them, and re-layouts: 3.51 us -> 0 us
    pallas_call x1, Pallas kernels: 111 us -> 105 us  [step(): pl.pallas_call(step_kernel, out_shape=(jax.ShapeDtypeStruct((rows_owned,...]
    unnamed x2 -> x0, local copies, waits for them, and re-layouts: 3.51 us -> none
    pallas_call x0 -> x1, Pallas kernels: none -> 1.98 us  [hand_on(): pl.pallas_call(hand_on_kernel, out_shape=(jax.ShapeDtypeStruct(mixed.shap...]
where the time goes in v4:
time: 109 us; the launch traced here: 108 us
  Pallas kernels  107 us (98%)
    pallas_call x1, Pallas kernels, step(): pl.pallas_call(step_kernel, out_shape=(jax.ShapeDtypeStruct((rows_owned,...  105 us

profile of v4, /device:TPU:14, one launch (start us, length us, event | category | flops | bytes accessed | tf_op | source)
XLA Modules:
  0.0 107.5 jit_solution(9954698406124432021)
XLA Ops:
  0.6 104.9 %step.1 = (bf16[160,2048]{1,0:T(8,128)(2,1)}, bf16[5,64,128]{2,1,0:T(8,128)(2,1)}) custom-call(s32[64]{0:T(128)} %lens.1, bf16[320,1024]{1,0:T(8,128)(2,1)} %queries.1, bf16[64,512,128]{2,1,0:T(8,128)(2,1)} %bitcast.5, bf16[64,512,128]{2,1,0:T(8,128)(2,1)} %bitcast.6, bf16[1024,2048]{1,0:T(8,128)(2,1)} %weight.1, bf16[320,128]{1,0:T(8,128)(2,1)} %fresh.1, ...), custom_call_target="tpu_custom_call" | custom-call | tf_op jit(solution)/shard_map/step/pallas_call | solution.py:559
  105.5 2.0 %hand_on.1 = (bf16[160,2048]{1,0:T(8,128)(2,1)}, bf16[5,64,128]{2,1,0:T(8,128)(2,1)}) custom-call(bf16[160,2048]{1,0:T(8,128)(2,1)} %get-tuple-element.6.mixed, bf16[5,64,128]{2,1,0:T(8,128)(2,1)} %get-tuple-element.7.moved), custom_call_target="tpu_custom_call" | custom-call | tf_op jit(solution)/shard_map/hand_on/pallas_call | solution.py:591

commit v5 on v4

--- a/solution.py
+++ b/solution.py
@@ -13,12 +13,13 @@
 WIDTHS = (512, 512, 512, 512)
 STARTS = tuple(sum(WIDTHS[:tree]) for tree in range(4))
 STEP_BASE = (0, 8, 12, 14)
-RECEIVES = ((7, 8, 9, 10), (8, 9, 10, 11))
-FIRST_UNIT = 3
+WORK = (
+    "C0", "C1", "S2", "S3", "K0", "K1", "D0", "N0", "C2", "N1", "F0", "C3",
+    "D1", "F1", "D2", "K2", "D3", "K3", "N2", "D4", "N3", "F2", "D5", "F3",
+    "D6", "D7", "A0", "B0", "A1", "B1", "A2", "B2", "A3", "B3",
+)
 CHUNKS = 4
 UNROLL = 8
-AHEAD = 3
-BACK = 2
 GATHER_KINDS = (
     "to_right", "to_left", "to_sibling", "share_right", "share_left", "share_far", "pass_left", "pass_right",
 )
@@ -42,8 +43,11 @@
     return y * 4 + z
 
 
-def within(number, low, high):
-    return jnp.logical_and(number >= low, number < high)
+def any_of(terms):
+    result = terms[0]
+    for term in terms[1:]:
+        result = jnp.logical_or(result, term)
+    return result
 
 
 def remote(source, target, send_sem, recv_sem, device):
@@ -319,7 +323,7 @@
 
         return carry
 
-    lax.fori_loop(0, AHEAD, send_first, 0)
+    lax.fori_loop(0, 2, send_first, 0)
 
     tokens = gathered.shape[2]
     half = gathered.shape[3] // 2
@@ -469,33 +473,25 @@
                     if rest % 2 == 1:
                         tree_message(tree, step + 1, phase, block, rest // 2)[0].start()
 
+    actions = {
+        "S": work.send_query,
+        "C": work.attend,
+        "K": lambda turn: publish(turn, work.combine(turn)),
+        "N": near,
+        "F": far,
+        "D": product_unit,
+    }
+
     def tick(time, carry):
-        @pl.when(within(time, 0, CHUNKS))
-        def _():
-            work.attend(time)
-
-            @pl.when(time + AHEAD < CHUNKS)
-            def _():
-                work.send_query(time + AHEAD)
-
-        @pl.when(within(time - BACK - 2, 0, CHUNKS))
-        def _():
-            far(time - BACK - 2)
-
-        @pl.when(within(time - BACK - 1, 0, CHUNKS))
-        def _():
-            near(time - BACK - 1)
-
-        @pl.when(within(time - BACK, 0, CHUNKS))
-        def _():
-            publish(time - BACK, work.combine(time - BACK))
-
-        @pl.when(within(time - FIRST_UNIT, 0, 8))
-        def _():
-            product_unit(time - FIRST_UNIT)
+        for kind, action in actions.items():
+            spots = [(spot, int(name[1])) for spot, name in enumerate(WORK) if name[0] == kind]
+
+            @pl.when(any_of([time == spot for spot, _ in spots]))
+            def _(action=action, spots=spots):
+                action(sum(jnp.where(time == spot, number, 0) for spot, number in spots))
 
         for step in range(4):
-            early, late = (FIRST_UNIT + RECEIVES[phase][step] for phase in range(2))
+            early, late = WORK.index(f"A{step}"), WORK.index(f"B{step}")
 
             @pl.when(jnp.logical_or(time == early, time == late))
             def _(step=step, late=late):
@@ -503,7 +499,7 @@
 
         return carry
 
-    lax.fori_loop(0, FIRST_UNIT + 15, tick, 0)
+    lax.fori_loop(0, len(WORK), tick, 0)
 
     own_parcel.wait()
     for step in range(1, 8):

time: 109 us -> 105 us (0.963); the launches traced: 108 us -> 105 us
  Pallas kernels: 107 us -> 104 us
    pallas_call x1, Pallas kernels: 105 us -> 102 us  [step(): pl.pallas_call(step_kernel, out_shape=(jax.ShapeDtypeStruct((rows_owned,...]
where the time goes in v5:
time: 105 us
  Pallas kernels  104 us (99%)
    pallas_call x1, Pallas kernels, step(): pl.pallas_call(step_kernel, out_shape=(jax.ShapeDtypeStruct((rows_owned,...  102 us

profile of v5, /device:TPU:14, one launch (start us, length us, event | category | flops | bytes accessed | tf_op | source)
XLA Modules:
  0.0 104.9 jit_solution(11925076671470091881)
XLA Ops:
  0.6 102.3 %step.1 = (bf16[160,2048]{1,0:T(8,128)(2,1)}, bf16[5,64,128]{2,1,0:T(8,128)(2,1)}) custom-call(s32[64]{0:T(128)} %lens.1, bf16[320,1024]{1,0:T(8,128)(2,1)} %queries.1, bf16[64,512,128]{2,1,0:T(8,128)(2,1)} %bitcast.5, bf16[64,512,128]{2,1,0:T(8,128)(2,1)} %bitcast.6, bf16[1024,2048]{1,0:T(8,128)(2,1)} %weight.1, bf16[320,128]{1,0:T(8,128)(2,1)} %fresh.1, ...), custom_call_target="tpu_custom_call" | custom-call | tf_op jit(solution)/shard_map/step/pallas_call | solution.py:555
  102.9 2.0 %hand_on.1 = (bf16[160,2048]{1,0:T(8,128)(2,1)}, bf16[5,64,128]{2,1,0:T(8,128)(2,1)}) custom-call(bf16[160,2048]{1,0:T(8,128)(2,1)} %get-tuple-element.6.mixed, bf16[5,64,128]{2,1,0:T(8,128)(2,1)} %get-tuple-element.7.moved), custom_call_target="tpu_custom_call" | custom-call | tf_op jit(solution)/shard_map/hand_on/pallas_call | solution.py:587

commit v6 on v5

--- a/solution.py
+++ b/solution.py
@@ -137,7 +137,7 @@
         even = self.side == 0
         fresh_keys = jnp.where(even, mine, theirs)
         fresh_values = jnp.where(even, theirs, mine)
-        scores = dot_nt(self.query_rows[turn].astype(jnp.bfloat16), fresh_keys)
+        scores = dot_nt(self.query_rows[turn, :rows, :].astype(jnp.bfloat16), fresh_keys)
         scores = jnp.where(fresh_valid, scores, masked_score)
         highest = jnp.max(scores, 1, keepdims=True)
         weights = jnp.exp2((scores - highest) * scale).astype(jnp.bfloat16)
@@ -145,7 +145,7 @@
             weights, jnp.concatenate([fresh_values, jnp.ones_like(fresh_values)], 1),
             preferred_element_type=jnp.float32,
         )
-        self.sum_fresh[...] = sums[:, :128]
+        self.sum_fresh[:rows, :] = sums[:, :128]
         self.mass_fresh[...] = sums[:, 128:]
         self.top_fresh[...] = jnp.broadcast_to(highest * scale, (rows, 128))
 
@@ -241,7 +241,7 @@
     bf16, f32 = jnp.bfloat16, jnp.float32
     dma = pltpu.SemaphoreType.DMA
     return [
-        pltpu.VMEM((CHUNKS, per * 40, 128), f32),
+        pltpu.VMEM((CHUNKS, per * 40 + 8, 128), f32),
         pltpu.VMEM((CHUNKS, per, 40, 128), bf16),
         pltpu.VMEM((CHUNKS, per, 40, 128), bf16),
         pltpu.VMEM((beams * 5, 128), bf16),
@@ -250,7 +250,7 @@
         pltpu.VMEM((CHUNKS, per * 40, 128), f32),
         pltpu.VMEM((CHUNKS, per * 40, 128), f32),
         pltpu.VMEM((CHUNKS, per * 40, 128), f32),
-        pltpu.VMEM((per * 40, 128), f32),
+        pltpu.VMEM((per * 40 + 8, 128), f32),
         pltpu.VMEM((per * 40, 128), f32),
         pltpu.VMEM((per * 40, 128), f32),
         pltpu.VMEM((CHUNKS, per, 40, 128), bf16),

time: 105 us -> 105 us (level)
  no operation moved by 1% of the time
where the time goes in v6:
time: 105 us
  Pallas kernels  104 us (99%)
    pallas_call x1, Pallas kernels, step(): pl.pallas_call(step_kernel, out_shape=(jax.ShapeDtypeStruct((rows_owned,...  102 us

profile of v6, /device:TPU:14, one launch (start us, length us, event | category | flops | bytes accessed | tf_op | source)
XLA Modules:
  0.0 104.9 jit_solution(11713643431663754926)
XLA Ops:
  0.6 102.3 %step.1 = (bf16[160,2048]{1,0:T(8,128)(2,1)}, bf16[5,64,128]{2,1,0:T(8,128)(2,1)}) custom-call(s32[64]{0:T(128)} %lens.1, bf16[320,1024]{1,0:T(8,128)(2,1)} %queries.1, bf16[64,512,128]{2,1,0:T(8,128)(2,1)} %bitcast.5, bf16[64,512,128]{2,1,0:T(8,128)(2,1)} %bitcast.6, bf16[1024,2048]{1,0:T(8,128)(2,1)} %weight.1, bf16[320,128]{1,0:T(8,128)(2,1)} %fresh.1, ...), custom_call_target="tpu_custom_call" | custom-call | tf_op jit(solution)/shard_map/step/pallas_call | solution.py:555
  102.9 2.0 %hand_on.1 = (bf16[160,2048]{1,0:T(8,128)(2,1)}, bf16[5,64,128]{2,1,0:T(8,128)(2,1)}) custom-call(bf16[160,2048]{1,0:T(8,128)(2,1)} %get-tuple-element.6.mixed, bf16[5,64,128]{2,1,0:T(8,128)(2,1)} %get-tuple-element.7.moved), custom_call_target="tpu_custom_call" | custom-call | tf_op jit(solution)/shard_map/hand_on/pallas_call | solution.py:587
